TPU v7x, 32 devices: a whole 2x2x4 slice. The times are simulated.
32 devices in a mesh: freq: 16 (over z, y, x), plane: 2 (over core).
Axes of the slice: x: 2, y: 2, z: 4, core: 2. Of those that a mesh axis runs over, the one named last changes fastest.
Arguments:
- state_in: float32 [2, 32, 5, 256, 128], P(None, 'freq', None, 'plane'), may hold values from -6 to 6
- forcing_in: float32 [2, 32, 5, 256, 128], P(None, 'freq', None, 'plane'), may hold values from -6 to 6
- base_flow: float32 [16, 5, 256, 128], P('freq', None, 'plane'), may hold values from -1 to 1
- station_index: int32 [2], replicated, may hold values from 0 to 15
- lobe_count: int32 [1], replicated, may hold values from 3 to 127
Outputs:
- state_out: float32 [2, 32, 5, 256, 128], P(None, 'freq', None, 'plane')
- forcing_out: float32 [2, 32, 5, 256, 128], P(None, 'freq', None, 'plane')
All inputs are finite; a program needn't handle non-finite values.
Results may differ from a plain program's by a relative error of at most 0.0003.
Values sent between devices are 32-bit elements; how exact they have to be, the bound alone decides.
A program may use at most 128 MiB of HBM per device.

v0:
```python
import functools
import math

import jax
import jax.numpy as jnp
import numpy as np
from jax import lax
from jax.experimental import pallas as pl
from jax.experimental.pallas import tpu as pltpu
from jax.sharding import PartitionSpec as P

SWEEPS = 4
STEPS = 2


SIDE_WEIGHT = 1.25
MARCH_WEIGHT = 4.0
DIAG_SHIFT = 4.0
ADVECT_SCALE = 0.5
BASE_SCALE = 0.5


def radial_tables(radius_count):
    indices = np.arange(radius_count)
    angles = math.pi * indices / (radius_count - 1)
    nodes = np.cos(angles)
    weights = np.where((indices == 0) | (indices == radius_count - 1), 2.0, 1.0)
    parity = 1.0 - 2.0 * ((indices[:, None] + indices[None, :]) % 2)
    offdiag = indices[:, None] != indices[None, :]
    spacing = np.where(offdiag, nodes[:, None] - nodes[None, :], 1.0)
    entries = np.where(offdiag, weights[:, None] / weights[None, :] * parity / spacing, 0.0)
    entries = entries - np.diag(entries.sum(axis=1))
    slopes = np.sin(angles)[:, None] * entries / (radius_count - 1)
    system = slopes.T @ slopes + DIAG_SHIFT * np.eye(radius_count)
    return slopes.astype(np.float32), np.linalg.inv(system).astype(np.float32)


def transform_tables(mode_ids, freqs, ntime):
    time_ids = np.arange(ntime)
    angles = 2.0 * math.pi * (mode_ids[:, None] * time_ids[None, :] % ntime) / ntime
    stacked = np.stack([np.cos(angles), -np.sin(angles)])
    return (
        (stacked / math.sqrt(freqs)).astype(np.float32),
        (stacked / math.sqrt(ntime)).astype(np.float32),
    )


def chevron(lobe_count, azimuths, start_az, total_az):
    position = start_az + jnp.arange(azimuths)
    phases = lobe_count[0] * position % total_az
    return 1.0 + 0.5 * jnp.cos(2.0 * math.pi * phases.astype(jnp.float32) / total_az)


def halves(x):
    high = x.astype(jnp.bfloat16)
    return high, (x - high.astype(jnp.float32)).astype(jnp.bfloat16)


def right_table(table):
    high, low = np_halves(table)
    return jnp.asarray(np.tile(np.concatenate([high, low], axis=1), (2, 1)))


def left_table(table):
    high, low = np_halves(table)
    return jnp.asarray(np.concatenate([high, high, low, low], axis=1))


def np_halves(table):
    high = table.astype(jnp.bfloat16)
    return high, (table - high.astype(np.float32)).astype(jnp.bfloat16)


def times_right(x, table):
    width = table.shape[1] // 2
    y = jnp.dot(jnp.concatenate(halves(x), axis=1), table, preferred_element_type=jnp.float32)
    return y[:, :width] + y[:, width:]


def times_left(table, x):
    high, low = halves(x)
    return jnp.dot(
        table,
        jnp.concatenate([high, low, high, low], axis=0),
        preferred_element_type=jnp.float32,
    )


def ring_of(f, p, nf, planes):
    at = f
    if nf % 4 == 0:
        high = nf // 4
        z, y, x = f // 4, (f // 2) % 2, f % 2
        column = 2 * y + (x + y) % 2
        at = column * high + z + (column % 2) * (high - 1 - 2 * z)
    return at * planes + p


def device_of(g, nf, planes):
    at = g // planes
    f = at
    if nf % 4 == 0:
        high = nf // 4
        column, z = at // high, at % high
        z = z + (column % 2) * (high - 1 - 2 * z)
        y = column // 2
        f = 4 * z + 2 * y + (column + y) % 2
    return f, g % planes


def march(
    dims,
    station_ref,
    shape_ref,
    rate_ref,
    state_ref,
    s_base,
    forcing_ref,
    far_omega,
    far_qt,
    far_st,
    far_inv,
    far_fwd,
    g_state,
    g_forcing,
    r_state,
    r_base,
    s_state,
    s_w,
    r_w,
    plane_w,
    x_one,
    b_one,
    edge_out,
    edge_in,
    x_ref,
    b_ref,
    f_ref,
    w_ref,
    o_state,
    o_forcing,
    send_sem,
    recv_sem,
    own_sem,
    halo_send,
    halo_recv,
    edge_send,
    edge_recv,
    load_sem,
    omega_ref,
    qt_ref,
    st_ref,
    inv_ref,
    fwd_ref,
    table_sem,
):
    nf, planes, own_az, variables, per_dev, radii, stored, rows, base_rows, w_rows = dims
    freqs = nf * per_dev
    span = nf * own_az
    runs = 2 * per_dev * variables
    ntime = inv_ref.shape[0]
    half = variables * freqs
    me = lax.axis_index("freq")
    plane = lax.axis_index("plane")
    ring = nf * planes
    here = ring_of(me, plane, nf, planes)
    part, block = here // nf, here % nf

    def named(device):
        return {"freq": device[0], "plane": device[1]}

    right_id = named(device_of((here + 1) % ring, nf, planes))
    left_id = named(device_of((here + ring - 1) % ring, nf, planes))
    barrier = pltpu.get_barrier_semaphore()

    @pl.loop(1, ring)
    def _(d):
        other = (me * planes + plane + d) % ring
        pl.semaphore_signal(
            barrier,
            inc=1,
            device_id={"freq": other // planes, "plane": other % planes},
            device_id_type=MESH,
        )

    beyond = {"freq": me, "plane": (plane + 1) % planes}
    behind = {"freq": me, "plane": (plane + planes - 1) % planes}
    load_state = pltpu.make_async_copy(state_ref, x_one.at[0, :, pl.ds(8, span), :], load_sem.at[0])
    load_forcing = pltpu.make_async_copy(forcing_ref, b_one, load_sem.at[1])
    load_state.start()
    load_forcing.start()
    tables = [
        pltpu.make_async_copy(far, near, table_sem.at[i])
        for i, (far, near) in enumerate(
            (
                (far_omega, omega_ref),
                (far_qt, qt_ref),
                (far_st, st_ref),
                (far_inv, inv_ref),
                (far_fwd, fwd_ref),
            )
        )
    ]
    for table in tables:
        table.start()
    pl.semaphore_wait(barrier, ring - 1)

    def owner(i):
        return device_of(plane * nf + i, nf, planes)

    def holder(i):
        return i, part

    def is_me(device):
        return (device[0] == me) & (device[1] == plane)

    def exchange(k, source, landing, target, origin, pick, mine, size, first):
        def rows_of(ref, i):
            return ref.at[pl.ds(pl.multiple_of(i * size, 8), size), :]

        def copy(i):
            return pltpu.make_async_remote_copy(
                src_ref=rows_of(source, pick(i)),
                dst_ref=rows_of(landing, mine),
                send_sem=send_sem.at[k, i],
                recv_sem=recv_sem.at[k, mine],
                device_id=named(target(i)),
                device_id_type=MESH,
            )

        def arrival(i):
            return pltpu.make_async_remote_copy(
                src_ref=rows_of(landing, i),
                dst_ref=rows_of(landing, i),
                send_sem=send_sem.at[k, i],
                recv_sem=recv_sem.at[k, i],
                device_id=named(origin(i)),
                device_id_type=MESH,
            )

        def own(i):
            return pltpu.make_async_copy(
                rows_of(source, pick(i)), rows_of(landing, mine), own_sem.at[k]
            )

        @pl.loop(0, nf)
        def _(d):
            i = (d + me) % nf
            stays = is_me(target(i))

            @pl.when(stays)
            def _():
                if first:
                    own(i).start()
                else:
                    own(i).wait()

            @pl.when(jnp.logical_not(stays))
            def _():
                if first:
                    copy(i).start()
                else:
                    copy(i).wait_send()

            if not first:

                @pl.when(jnp.logical_not(is_me(origin(i))))
                def _():
                    arrival(i).wait_recv()

    def same(i):
        return i

    base_args = (1, s_base, r_base, owner, holder, same, me, base_rows)
    state_args = (0, s_state, r_state, owner, holder, same, me, rows)
    w_args = (2, s_w, r_w, holder, owner, lambda i: 0, block, w_rows)
    out_state_args = (3, o_state, g_state, holder, owner, same, block, rows)
    out_forcing_args = (4, o_forcing, g_forcing, holder, owner, same, block, rows)
    exchange(*base_args, True)

    def halo_copies(e):
        slot = e % 2
        return (
            pltpu.make_async_remote_copy(
                src_ref=x_ref.at[slot, own_az],
                dst_ref=x_ref.at[slot, 0],
                send_sem=halo_send.at[0, e],
                recv_sem=halo_recv.at[0, e],
                device_id=right_id,
                device_id_type=MESH,
            ),
            pltpu.make_async_remote_copy(
                src_ref=x_ref.at[slot, 1],
                dst_ref=x_ref.at[slot, own_az + 1],
                send_sem=halo_send.at[1, e],
                recv_sem=halo_recv.at[1, e],
                device_id=left_id,
                device_id_type=MESH,
            ),
        )

    def place(a, c, v, kk):
        return ((c * variables + v) * per_dev + kk) * nf

    def packed_row(a, c, v, kk):
        return ((c * per_dev + kk) * variables + v) * own_az + a

    def each_run(visit):
        @pl.loop(0, own_az)
        def _(a):
            for c in range(2):
                for v in range(variables):
                    for kk in range(per_dev):
                        visit(a, place(a, c, v, kk), packed_row(a, c, v, kk))

    def in_row(a, c, v, kk):
        return ((c * per_dev + kk) * variables + v) * own_az + a

    def edge_copies(e):
        return [
            pltpu.make_async_remote_copy(
                src_ref=edge_out.at[e, side],
                dst_ref=edge_in.at[e, side],
                send_sem=edge_send.at[side, e],
                recv_sem=edge_recv.at[side, e],
                device_id=target,
                device_id_type=MESH,
            )
            for side, target in ((0, beyond), (1, behind))
        ]

    def send_edges(slot, e):
        for m in range(runs):
            edge_out[e, 0, pl.ds(m, 1), :] = x_one[slot, m, pl.ds(7 + span, 1), :]
            edge_out[e, 1, pl.ds(m, 1), :] = x_one[slot, m, pl.ds(8, 1), :]
        for copy in edge_copies(e):
            copy.start()

    for table in tables:
        table.wait()
    load_state.wait()
    send_edges(0, 0)
    load_forcing.wait()

    @pl.loop(0, runs)
    def _(m):
        b_one[m] = MARCH_WEIGHT * x_one[0, m, pl.ds(8, span), :] + b_one[m]

    exchange(*base_args, False)
    for station in range(STEPS):
        wanted = station_ref[station]

        @pl.loop(0, own_az)
        def _(a):
            for v in range(variables):
                scaled = (BASE_SCALE * shape_ref[a]) * r_base[
                    pl.ds(
                        (wanted // stored) * base_rows
                        + ((wanted % stored) * variables + v) * own_az
                        + a,
                        1,
                    ),
                    :,
                ]
                if station == 0:
                    s_w[pl.ds(v * own_az + a, 1), :] = scaled
                else:
                    w_ref[(station - 1) * own_az + a, pl.ds(v, 1), :] = scaled

        if station == 0:
            exchange(*w_args, True)
    exchange(*w_args, False)

    @pl.loop(0, nf)
    def _(j):
        for v in range(variables):
            plane_w[v, pl.ds(j * own_az, own_az), :] = r_w[pl.ds(j * w_rows + v * own_az, own_az), :]

    @pl.loop(0, SWEEPS)
    def _(e):
        src, dst = e % 2, (e + 1) % 2
        for copy in edge_copies(e):
            copy.wait()
        for m in range(runs):
            x_one[src, m, pl.ds(7, 1), :] = edge_in[e, 0, pl.ds(m, 1), :]
            x_one[src, m, pl.ds(8 + span, 1), :] = edge_in[e, 1, pl.ds(m, 1), :]
        for kk in range(per_dev):
            rate = rate_ref[kk]

            @pl.loop(0, variables)
            def _(v):
                w = plane_w[v]
                at = [(c * per_dev + kk) * variables + v for c in range(2)]
                real, imag = [x_one[src, m, pl.ds(8, span), :] for m in at]
                mixing = (w * real - rate * imag, w * imag + rate * real)
                summed = [
                    SIDE_WEIGHT
                    * (x_one[src, m, pl.ds(7, span), :] + x_one[src, m, pl.ds(9, span), :])
                    + b_one[m]
                    - mixed
                    for m, mixed in zip(at, mixing)
                ]
                q = times_right(jnp.concatenate(summed, axis=0), qt_ref[...])
                x_one[dst, at[0], pl.ds(8, span), :] = q[:span]
                x_one[dst, at[1], pl.ds(8, span), :] = q[span:]

        @pl.when(e < SWEEPS - 1)
        def _():
            send_edges(dst, e + 1)

    settled = SWEEPS % 2

    @pl.loop(0, nf)
    def _(j):
        for m in range(runs):
            s_state[pl.ds(j * rows + m * own_az, own_az), :] = x_one[
                settled, m, pl.ds(8 + j * own_az, own_az), :
            ]

    exchange(*state_args, True)
    exchange(*state_args, False)

    def unpack_state(a, start, row):
        x_ref[0, a + 1, pl.ds(start, nf), :] = r_state[pl.ds(row, nf, stride=rows), :]

    each_run(unpack_state)
    for copy in halo_copies(0):
        copy.start()
    omega = omega_ref[...][None]
    flat = (2 * half, radii)
    cube = (variables, freqs, radii)

    def sweep_slab(src, dst, a, station):
        x = x_ref[src, a + 1]
        beside = SIDE_WEIGHT * (x_ref[src, a] + x_ref[src, a + 2]) + b_ref[a]
        real, imag = x[:half].reshape(cube), x[half:].reshape(cube)
        w = w_ref[(station - 1) * own_az + a][:variables][:, None, :]
        mixing = jnp.concatenate([w * real - omega * imag, w * imag + omega * real], axis=0)
        summed = beside - mixing.reshape(flat)
        x_ref[dst, a + 1] = times_right(summed, qt_ref[...])

    def advect_slab(slot, a, final):
        x = x_ref[slot, a + 1]
        beside = 0.5 * (x_ref[slot, a + 2] - x_ref[slot, a])

        def lanes(y):
            return [
                jnp.concatenate(
                    [
                        y[v * freqs : (v + 1) * freqs],
                        y[half + v * freqs : half + (v + 1) * freqs],
                    ],
                    axis=0,
                )
                for v in range(variables)
            ]

        both = jnp.concatenate(lanes(x) + lanes(beside), axis=1)
        in_time = times_left(inv_ref[...], both)
        u = [in_time[:, v * radii : (v + 1) * radii] for v in range(variables)]
        ua = [
            in_time[:, (variables + v) * radii : (variables + v + 1) * radii]
            for v in range(variables)
        ]
        radial = times_right(jnp.concatenate(u, axis=0), st_ref[...])
        ur = [radial[v * ntime : (v + 1) * ntime] for v in range(variables)]
        n = [u[1] * ur[v] + u[2] * ua[v] for v in range(variables)]
        n[0] = n[0] + u[0] * (ur[1] + ua[2])
        source = -ADVECT_SCALE * jnp.concatenate(n, axis=1)
        spectral = times_left(fwd_ref[...], source)
        forcing = jnp.concatenate(
            [
                spectral[c * freqs : (c + 1) * freqs, v * radii : (v + 1) * radii]
                for c in range(2)
                for v in range(variables)
            ],
            axis=0,
        )
        if final:
            f_ref[a] = forcing
        else:
            b_ref[a] = MARCH_WEIGHT * x + forcing

    def advect_all(slot, e, final):
        @pl.loop(1, own_az - 1)
        def _(a):
            advect_slab(slot, a, final)

        for copy in halo_copies(e):
            copy.wait()
        advect_slab(slot, 0, final)
        if own_az > 1:
            advect_slab(slot, own_az - 1, final)

    advect_all(0, 0, False)
    for station in range(1, STEPS):

        @pl.loop(0, SWEEPS)
        def _(sweep):
            e = (station - 1) * SWEEPS + sweep
            src, dst = e % 2, (e + 1) % 2

            @pl.when(sweep > 0)
            def _():
                for copy in halo_copies(e):
                    copy.wait()

            sweep_slab(src, dst, 0, station)
            if own_az > 1:
                sweep_slab(src, dst, own_az - 1, station)
            for copy in halo_copies(e + 1):
                copy.start()

            @pl.loop(1, own_az - 1)
            def _(a):
                sweep_slab(src, dst, a, station)

        last = station * SWEEPS
        slot = last % 2
        final = station == STEPS - 1
        if final:

            def pack_state(a, start, row):
                o_state[pl.ds(row, nf, stride=rows), :] = x_ref[slot, a + 1, pl.ds(start, nf), :]

            each_run(pack_state)
            exchange(*out_state_args, True)

        advect_all(slot, last, final)

    def pack_forcing(a, start, row):
        o_forcing[pl.ds(row, nf, stride=rows), :] = f_ref[a, pl.ds(start, nf), :]

    each_run(pack_forcing)
    exchange(*out_forcing_args, True)
    exchange(*out_state_args, False)
    exchange(*out_forcing_args, False)


def per_device(state_in, forcing_in, base_flow, station_index, lobe_count):
    _, per_dev, variables, span_az, radii = state_in.shape
    nf = lax.axis_size("freq")
    planes = lax.axis_size("plane")
    freqs = per_dev * nf
    ntime = 3 * freqs // 2
    own_az = span_az // nf
    stored = base_flow.shape[0]
    slopes, inverse_p = radial_tables(radii)
    mode_ids = (np.arange(nf)[None, :] * per_dev + np.arange(per_dev)[:, None]).reshape(-1)
    inverse, forward = transform_tables(mode_ids, freqs, ntime)
    omegas = np.broadcast_to((0.5 * mode_ids / freqs).astype(np.float32)[:, None], (freqs, radii))
    plane = lax.axis_index("plane")
    here = ring_of(lax.axis_index("freq"), plane, nf, planes)
    shape_az = chevron(lobe_count, own_az, here * own_az, span_az * planes)

    def padded_rows(count):
        return -(-count // 8) * 8

    def chunks(x, size):
        x = x.reshape(-1, nf, own_az, radii).transpose(1, 0, 2, 3).reshape(nf, -1, radii)
        x = jnp.pad(x, ((0, 0), (0, size - x.shape[1]), (0, 0)))
        return x.reshape(nf * size, radii)

    count = 2 * per_dev * variables * own_az
    rows = padded_rows(count)
    base_rows = padded_rows(stored * variables * own_az)
    w_rows = padded_rows(variables * own_az)
    dims = (nf, planes, own_az, variables, per_dev, radii, stored, rows, base_rows, w_rows)
    half = variables * freqs
    exchanges = (STEPS - 1) * SWEEPS + 1
    runs = 2 * per_dev * variables
    edge_rows = padded_rows(runs)
    first_mode = lax.axis_index("freq") * per_dev
    rates = 0.5 * (first_mode + jnp.arange(per_dev)).astype(jnp.float32) / freqs
    smem = pl.BlockSpec(memory_space=pltpu.SMEM)
    anywhere = pl.BlockSpec(memory_space=pl.ANY)
    packed = (nf * rows, radii)
    f32 = jnp.float32
    outs = pl.pallas_call(
        functools.partial(march, dims),
        out_shape=[jax.ShapeDtypeStruct(packed, f32)] * 2,
        in_specs=[smem, smem, smem, anywhere, anywhere, anywhere] + [anywhere] * 5,
        out_specs=[anywhere, anywhere],
        scratch_shapes=[
            pltpu.VMEM(packed, f32),
            pltpu.VMEM((nf * base_rows, radii), f32),
            pltpu.VMEM(packed, f32),
            pltpu.VMEM((w_rows, radii), f32),
            pltpu.VMEM((nf * w_rows, radii), f32),
            pltpu.VMEM((variables, span_az, radii), f32),
            pltpu.VMEM((2, runs, span_az + 16, radii), f32),
            pltpu.VMEM((runs, span_az, radii), f32),
            pltpu.VMEM((SWEEPS, 2, edge_rows, radii), f32),
            pltpu.VMEM((SWEEPS, 2, edge_rows, radii), f32),
            pltpu.VMEM((2, own_az + 2, 2 * half, radii), f32),
            pltpu.VMEM((own_az, 2 * half, radii), f32),
            pltpu.VMEM((own_az, 2 * half, radii), f32),
            pltpu.VMEM(((STEPS - 1) * own_az, padded_rows(variables), radii), f32),
            pltpu.VMEM(packed, f32),
            pltpu.VMEM(packed, f32),
            pltpu.SemaphoreType.DMA((5, nf)),
            pltpu.SemaphoreType.DMA((5, nf)),
            pltpu.SemaphoreType.DMA((5,)),
            pltpu.SemaphoreType.DMA((2, exchanges)),
            pltpu.SemaphoreType.DMA((2, exchanges)),
            pltpu.SemaphoreType.DMA((2, SWEEPS)),
            pltpu.SemaphoreType.DMA((2, SWEEPS)),
            pltpu.SemaphoreType.DMA((2,)),
            pltpu.VMEM((freqs, radii), f32),
            pltpu.VMEM((2 * radii, 2 * radii), jnp.bfloat16),
            pltpu.VMEM((2 * radii, 2 * radii), jnp.bfloat16),
            pltpu.VMEM((ntime, 8 * freqs), jnp.bfloat16),
            pltpu.VMEM((2 * freqs, 4 * ntime), jnp.bfloat16),
            pltpu.SemaphoreType.DMA((5,)),
        ],
        compiler_params=pltpu.CompilerParams(
            collective_id=0, has_side_effects=True, vmem_limit_bytes=63_000 * 1024
        ),
    )(
        station_index,
        shape_az,
        rates,
        state_in.reshape(runs, span_az, radii),
        chunks(base_flow, base_rows),
        forcing_in.reshape(runs, span_az, radii),
        jnp.asarray(omegas),
        right_table(inverse_p.T),
        right_table(slopes.T),
        left_table(inverse.transpose(2, 0, 1).reshape(ntime, 2 * freqs)),
        left_table(forward.reshape(2 * freqs, ntime)),
    )

    return tuple(finish(y, nf, per_dev, variables, own_az, radii, rows, count) for y in outs)


def finish(y, nf, per_dev, variables, own_az, radii, rows, count):
    y = y.reshape(nf, rows, radii)[:, :count].reshape(nf, -1, own_az, radii)
    return y.transpose(1, 0, 2, 3).reshape(2, per_dev, variables, nf * own_az, radii)


MESH = pl.DeviceIdType.MESH


def solution(mesh):
    return jax.shard_map(
        per_device,
        mesh=mesh,
        in_specs=(
            P(None, "freq", None, "plane", None),
            P(None, "freq", None, "plane", None),
            P("freq", None, "plane", None),
            P(),
            P(),
        ),
        out_specs=(P(None, "freq", None, "plane", None), P(None, "freq", None, "plane", None)),
        check_vma=False,
    )
```

profile of v0, /device:TPU:30, one launch (start us, length us, event | category | flops | bytes accessed | tf_op | source)
XLA Modules:
  0.0 155.8 jit_solution(11956324473388836216)
XLA Ops:
  1.4 0.6 fusion.4.shape_ref
  1.9 0.6 convert_multiply_fusion.rate_ref
  2.5 1.7 %copy.12 = f32[5,16,8,128]{3,2,0,1:T(8,128)} copy(f32[5,16,8,128]{3,2,1,0:T(8,128)} %bitcast.23) | data formatting | bytes 655360 | tf_op jit(solution)/shard_map/reshape | solution.py:560
  4.2 1.3 jit_solution_.3.far_omega
  5.5 146.4 %shard_map.113 = (f32[2560,128]{1,0:T(8,128)}, f32[2560,128]{1,0:T(8,128)}) custom-call(s32[2]{0:T(128)} %station_ref.1, f32[8]{0:T(128)} %fusion.4.shape_ref, f32[2]{0:T(128)} %convert_multiply_fusion.rate_ref, f32[20,128,128]{2,1,0:T(8,128)} %bitcast.16, f32[640,128]{1,0:T(8,128)} %bitcast.18, f32[20,128,128]{2,1,0:T(8,128)} %bitcast.17, ...), custom_call_target="tpu_custom_call" | custom-call | tf_op jit(solution)/shard_map/pallas_call | solution.py:579
  152.0 0.0 copy-start
  152.0 2.6 %copy.13 = f32[20,16,8,128]{3,2,1,0:T(8,128)} copy(f32[20,16,8,128]{3,2,0,1:T(8,128)} %bitcast.20) | data formatting | bytes 2621440 | tf_op jit(solution)/shard_map/transpose | solution.py:638
  154.6 0.0 copy-done
  154.6 1.2 copy.14
Async XLA Ops:
  152.0 2.6 %copy-start = (f32[2560,128]{1,0:T(8,128)S(1)}, f32[2560,128]{1,0:T(8,128)}, u32[]{:S(2)}) copy-start(f32[2560,128]{1,0:T(8,128)} %get-tuple-element.5) | copy-start | bytes 3932164
where the time goes:
time: 157 us; the launch traced here: 156 us
  Pallas kernels  146 us (93%)
  local copies, waits for them, and re-layouts  6.87 us (4%)
    pallas_call x1, Pallas kernels, per_device(): pl.pallas_call(functools.partial(march, dims), out_shape=[jax.ShapeDtypeS...  146 us
    transpose x2, local copies, waits for them, and re-layouts, finish(): y.transpose(1, 0, 2, 3).reshape(2, per_dev, variables, nf * own_az, radii)  3.82 us

commit v1 on v0

--- a/solution.py
+++ b/solution.py
@@ -638,12 +638,523 @@
     return y.transpose(1, 0, 2, 3).reshape(2, per_dev, variables, nf * own_az, radii)
 
 
+def relay(
+    dims,
+    station_ref,
+    lobe_ref,
+    state_ref,
+    base_ref,
+    forcing_ref,
+    far_qt,
+    far_st,
+    far_inv,
+    far_fwd,
+    g_state,
+    g_forcing,
+    r_state,
+    r_base,
+    s_w,
+    plane_w,
+    x_one,
+    b_one,
+    edge_out,
+    edge_in,
+    x_ref,
+    b_ref,
+    f_ref,
+    w_ref,
+    o_march,
+    o_forcing,
+    send_sem,
+    recv_sem,
+    own_sem,
+    halo_send,
+    halo_recv,
+    edge_send,
+    edge_recv,
+    load_sem,
+    omega_ref,
+    qt_ref,
+    st_ref,
+    inv_ref,
+    fwd_ref,
+    table_sem,
+):
+    nf, planes, own_az, variables, per_dev, radii, stored = dims
+    freqs = nf * per_dev
+    span = nf * own_az
+    runs = 2 * per_dev * variables
+    ntime = inv_ref.shape[0]
+    half = variables * freqs
+    me = lax.axis_index("freq")
+    plane = lax.axis_index("plane")
+    ring = nf * planes
+    here = ring_of(me, plane, nf, planes)
+    part, block = here // nf, here % nf
+
+    def named(device):
+        return {"freq": device[0], "plane": device[1]}
+
+    right_id = named(device_of((here + 1) % ring, nf, planes))
+    left_id = named(device_of((here + ring - 1) % ring, nf, planes))
+    barrier = pltpu.get_barrier_semaphore()
+
+    @pl.loop(1, ring)
+    def _(d):
+        other = (me * planes + plane + d) % ring
+        pl.semaphore_signal(
+            barrier,
+            inc=1,
+            device_id={"freq": other // planes, "plane": other % planes},
+            device_id_type=MESH,
+        )
+
+    beyond = {"freq": me, "plane": (plane + 1) % planes}
+    behind = {"freq": me, "plane": (plane + planes - 1) % planes}
+    load_state = pltpu.make_async_copy(state_ref, x_one.at[0, :, pl.ds(8, span), :], load_sem.at[0])
+    load_forcing = pltpu.make_async_copy(forcing_ref, b_one, load_sem.at[1])
+    load_state.start()
+    load_forcing.start()
+    tables = [
+        pltpu.make_async_copy(far, near, table_sem.at[i])
+        for i, (far, near) in enumerate(
+            ((far_qt, qt_ref), (far_st, st_ref), (far_inv, inv_ref), (far_fwd, fwd_ref))
+        )
+    ]
+    for table in tables:
+        table.start()
+    pl.semaphore_wait(barrier, ring - 1)
+
+    def owner(i):
+        return device_of(plane * nf + i, nf, planes)
+
+    def holder(i):
+        return i, part
+
+    def is_me(device):
+        return (device[0] == me) & (device[1] == plane)
+
+    def azimuths(i):
+        return pl.ds(pl.multiple_of(i * own_az, 8), own_az)
+
+    def exchange(k, piece, landing, target, origin, mine):
+        def copy(i):
+            return pltpu.make_async_remote_copy(
+                src_ref=piece(i),
+                dst_ref=landing(mine),
+                send_sem=send_sem.at[k, i],
+                recv_sem=recv_sem.at[k, mine],
+                device_id=named(target(i)),
+                device_id_type=MESH,
+            )
+
+        def arrival(i):
+            return pltpu.make_async_remote_copy(
+                src_ref=landing(i),
+                dst_ref=landing(i),
+                send_sem=send_sem.at[k, i],
+                recv_sem=recv_sem.at[k, i],
+                device_id=named(origin(i)),
+                device_id_type=MESH,
+            )
+
+        def own(i):
+            return pltpu.make_async_copy(piece(i), landing(mine), own_sem.at[k])
+
+        def start():
+            @pl.loop(0, nf)
+            def _(d):
+                i = (d + me) % nf
+                stays = is_me(target(i))
+
+                @pl.when(stays)
+                def _():
+                    own(i).start()
+
+                @pl.when(jnp.logical_not(stays))
+                def _():
+                    copy(i).start()
+
+        def wait():
+            @pl.loop(0, nf)
+            def _(d):
+                i = (d + me) % nf
+                stays = is_me(target(i))
+
+                @pl.when(stays)
+                def _():
+                    own(i).wait()
+
+                @pl.when(jnp.logical_not(stays))
+                def _():
+                    copy(i).wait_send()
+
+                @pl.when(jnp.logical_not(is_me(origin(i))))
+                def _():
+                    arrival(i).wait_recv()
+
+        return start, wait
+
+    base_start, base_wait = exchange(
+        0,
+        lambda i: base_ref.at[:, azimuths(i), :],
+        lambda j: r_base.at[j],
+        owner,
+        holder,
+        me,
+    )
+    w_moves = [
+        exchange(
+            1 + s,
+            lambda i, s=s: s_w.at[s],
+            lambda j, s=s: plane_w.at[s, :, azimuths(j), :],
+            holder,
+            owner,
+            block,
+        )
+        for s in range(STEPS)
+    ]
+    settled = SWEEPS % 2
+    state_start, state_wait = exchange(
+        1 + STEPS,
+        lambda i: x_one.at[settled, :, pl.ds(pl.multiple_of(8 + i * own_az, 8), own_az), :],
+        lambda j: r_state.at[j],
+        owner,
+        holder,
+        me,
+    )
+    march_start, march_wait = exchange(
+        2 + STEPS,
+        lambda i: o_march.at[i],
+        lambda j: b_one.at[:, azimuths(j), :],
+        holder,
+        owner,
+        block,
+    )
+    forcing_start, forcing_wait = exchange(
+        3 + STEPS,
+        lambda i: o_forcing.at[i],
+        lambda j: g_forcing.at[:, azimuths(j), :],
+        holder,
+        owner,
+        block,
+    )
+    base_start()
+
+    def halo_copies(e):
+        slot = e % 2
+        return (
+            pltpu.make_async_remote_copy(
+                src_ref=x_ref.at[slot, own_az],
+                dst_ref=x_ref.at[slot, 0],
+                send_sem=halo_send.at[0, e],
+                recv_sem=halo_recv.at[0, e],
+                device_id=right_id,
+                device_id_type=MESH,
+            ),
+            pltpu.make_async_remote_copy(
+                src_ref=x_ref.at[slot, 1],
+                dst_ref=x_ref.at[slot, own_az + 1],
+                send_sem=halo_send.at[1, e],
+                recv_sem=halo_recv.at[1, e],
+                device_id=left_id,
+                device_id_type=MESH,
+            ),
+        )
+
+    def each_run(visit):
+        @pl.loop(0, own_az)
+        def _(a):
+            for c in range(2):
+                for v in range(variables):
+                    for kk in range(per_dev):
+                        start = ((c * variables + v) * per_dev + kk) * nf
+                        visit(a, start, (c * per_dev + kk) * variables + v)
+
+    def edge_copies(e):
+        return [
+            pltpu.make_async_remote_copy(
+                src_ref=edge_out.at[e, side],
+                dst_ref=edge_in.at[e, side],
+                send_sem=edge_send.at[side, e],
+                recv_sem=edge_recv.at[side, e],
+                device_id=target,
+                device_id_type=MESH,
+            )
+            for side, target in ((0, beyond), (1, behind))
+        ]
+
+    def send_edges(slot, e):
+        for m in range(runs):
+            edge_out[e, 0, pl.ds(m, 1), :] = x_one[slot, m, pl.ds(7 + span, 1), :]
+            edge_out[e, 1, pl.ds(m, 1), :] = x_one[slot, m, pl.ds(8, 1), :]
+        for copy in edge_copies(e):
+            copy.start()
+
+    for kk in range(per_dev):
+        modes = lax.broadcasted_iota(jnp.int32, (nf, radii), 0) * per_dev + kk
+        omega_ref[pl.ds(kk * nf, nf), :] = 0.5 * modes.astype(jnp.float32) / freqs
+    load_state.wait()
+    send_edges(0, 0)
+    load_forcing.wait()
+
+    @pl.loop(0, runs)
+    def _(m):
+        b_one[m] = MARCH_WEIGHT * x_one[0, m, pl.ds(8, span), :] + b_one[m]
+
+    for table in tables:
+        table.wait()
+    position = here * own_az + lax.broadcasted_iota(jnp.int32, (own_az, radii), 0)
+    phases = (lobe_ref[0] * position) % (span * planes)
+    shape = 1.0 + 0.5 * jnp.cos(2.0 * math.pi * phases.astype(jnp.float32) / (span * planes))
+    base_wait()
+    for station in range(STEPS):
+        wanted = station_ref[station]
+        for v in range(variables):
+            scaled = (BASE_SCALE * shape) * r_base[
+                wanted // stored, (wanted % stored) * variables + v
+            ]
+            s_w[station, v] = scaled
+            if station > 0:
+                for a in range(own_az):
+                    w_ref[(station - 1) * own_az + a, pl.ds(v, 1), :] = scaled[a : a + 1]
+        w_moves[station][0]()
+
+    def freq_sweeps(station):
+        @pl.loop(0, SWEEPS)
+        def _(sweep):
+            e = station * SWEEPS + sweep
+            src, dst = e % 2, (e + 1) % 2
+            for copy in edge_copies(e):
+                copy.wait()
+            for m in range(runs):
+                x_one[src, m, pl.ds(7, 1), :] = edge_in[e, 0, pl.ds(m, 1), :]
+                x_one[src, m, pl.ds(8 + span, 1), :] = edge_in[e, 1, pl.ds(m, 1), :]
+            for kk in range(per_dev):
+                rate = (me * per_dev + kk).astype(jnp.float32) * (0.5 / freqs)
+
+                @pl.loop(0, variables)
+                def _(v):
+                    w = plane_w[station, v]
+                    at = [(c * per_dev + kk) * variables + v for c in range(2)]
+                    real, imag = [x_one[src, m, pl.ds(8, span), :] for m in at]
+                    mixing = (w * real - rate * imag, w * imag + rate * real)
+                    summed = [
+                        SIDE_WEIGHT
+                        * (x_one[src, m, pl.ds(7, span), :] + x_one[src, m, pl.ds(9, span), :])
+                        + b_one[m]
+                        - mixed
+                        for m, mixed in zip(at, mixing)
+                    ]
+                    q = times_right(jnp.concatenate(summed, axis=0), qt_ref[...])
+                    x_one[dst, at[0], pl.ds(8, span), :] = q[:span]
+                    x_one[dst, at[1], pl.ds(8, span), :] = q[span:]
+
+            @pl.when(e < STEPS * SWEEPS - 1)
+            def _():
+                send_edges(dst, e + 1)
+
+    w_moves[0][1]()
+    freq_sweeps(0)
+    state_start()
+    state_wait()
+
+    def unpack_state(a, start, m):
+        x_ref[0, a + 1, pl.ds(start, nf), :] = r_state[:, m, a, :]
+
+    each_run(unpack_state)
+    for copy in halo_copies(0):
+        copy.start()
+    omega = omega_ref[...][None]
+    flat = (2 * half, radii)
+    cube = (variables, freqs, radii)
+
+    def sweep_slab(src, dst, a, station):
+        x = x_ref[src, a + 1]
+        beside = SIDE_WEIGHT * (x_ref[src, a] + x_ref[src, a + 2]) + b_ref[a]
+        real, imag = x[:half].reshape(cube), x[half:].reshape(cube)
+        w = w_ref[(station - 1) * own_az + a][:variables][:, None, :]
+        mixing = jnp.concatenate([w * real - omega * imag, w * imag + omega * real], axis=0)
+        summed = beside - mixing.reshape(flat)
+        x_ref[dst, a + 1] = times_right(summed, qt_ref[...])
+
+    def advect_slab(slot, a, final):
+        x = x_ref[slot, a + 1]
+        beside = 0.5 * (x_ref[slot, a + 2] - x_ref[slot, a])
+
+        def lanes(y):
+            return [
+                jnp.concatenate(
+                    [
+                        y[v * freqs : (v + 1) * freqs],
+                        y[half + v * freqs : half + (v + 1) * freqs],
+                    ],
+                    axis=0,
+                )
+                for v in range(variables)
+            ]
+
+        both = jnp.concatenate(lanes(x) + lanes(beside), axis=1)
+        in_time = times_left(inv_ref[...], both)
+        u = [in_time[:, v * radii : (v + 1) * radii] for v in range(variables)]
+        ua = [
+            in_time[:, (variables + v) * radii : (variables + v + 1) * radii]
+            for v in range(variables)
+        ]
+        radial = times_right(jnp.concatenate(u, axis=0), st_ref[...])
+        ur = [radial[v * ntime : (v + 1) * ntime] for v in range(variables)]
+        n = [u[1] * ur[v] + u[2] * ua[v] for v in range(variables)]
+        n[0] = n[0] + u[0] * (ur[1] + ua[2])
+        source = -ADVECT_SCALE * jnp.concatenate(n, axis=1)
+        spectral = times_left(fwd_ref[...], source)
+        forcing = jnp.concatenate(
+            [
+                spectral[c * freqs : (c + 1) * freqs, v * radii : (v + 1) * radii]
+                for c in range(2)
+                for v in range(variables)
+            ],
+            axis=0,
+        )
+        if final:
+            f_ref[a] = forcing
+        else:
+            b_ref[a] = MARCH_WEIGHT * x + forcing
+
+    def advect_all(slot, e, final):
+        @pl.loop(1, own_az - 1)
+        def _(a):
+            advect_slab(slot, a, final)
+
+        for copy in halo_copies(e):
+            copy.wait()
+        advect_slab(slot, 0, final)
+        advect_slab(slot, own_az - 1, final)
+
+    def pack_march(a, start, m):
+        o_march[:, m, a, :] = b_ref[a, pl.ds(start, nf), :]
+
+    def pack_forcing(a, start, m):
+        o_forcing[:, m, a, :] = f_ref[a, pl.ds(start, nf), :]
+
+    advect_all(0, 0, False)
+    each_run(pack_march)
+    march_start()
+
+    @pl.loop(0, SWEEPS)
+    def _(e):
+        src, dst = e % 2, (e + 1) % 2
+
+        @pl.when(e > 0)
+        def _():
+            for copy in halo_copies(e):
+                copy.wait()
+
+        sweep_slab(src, dst, 0, 1)
+        sweep_slab(src, dst, own_az - 1, 1)
+        for copy in halo_copies(e + 1):
+            copy.start()
+
+        @pl.loop(1, own_az - 1)
+        def _(a):
+            sweep_slab(src, dst, a, 1)
+
+    advect_all(SWEEPS % 2, SWEEPS, True)
+    each_run(pack_forcing)
+    march_wait()
+    forcing_start()
+    w_moves[1][1]()
+    freq_sweeps(1)
+    out_state = pltpu.make_async_copy(
+        x_one.at[(2 * SWEEPS) % 2, :, pl.ds(8, span), :], g_state, load_sem.at[0]
+    )
+    out_state.start()
+    out_state.wait()
+    forcing_wait()
+
+
+def per_device_tiled(state_in, forcing_in, base_flow, station_index, lobe_count):
+    _, per_dev, variables, span_az, radii = state_in.shape
+    nf = lax.axis_size("freq")
+    planes = lax.axis_size("plane")
+    freqs = per_dev * nf
+    ntime = 3 * freqs // 2
+    own_az = span_az // nf
+    stored = base_flow.shape[0]
+    slopes, inverse_p = radial_tables(radii)
+    mode_ids = (np.arange(nf)[None, :] * per_dev + np.arange(per_dev)[:, None]).reshape(-1)
+    inverse, forward = transform_tables(mode_ids, freqs, ntime)
+    dims = (nf, planes, own_az, variables, per_dev, radii, stored)
+    half = variables * freqs
+    runs = 2 * per_dev * variables
+    edge_rows = -(-runs // 8) * 8
+    rounds = STEPS * SWEEPS
+    smem = pl.BlockSpec(memory_space=pltpu.SMEM)
+    anywhere = pl.BlockSpec(memory_space=pl.ANY)
+    f32 = jnp.float32
+    pieces = (nf, runs, own_az, radii)
+    outs = pl.pallas_call(
+        functools.partial(relay, dims),
+        out_shape=[jax.ShapeDtypeStruct((runs, span_az, radii), f32)] * 2,
+        in_specs=[smem, smem] + [anywhere] * 7,
+        out_specs=[anywhere, anywhere],
+        scratch_shapes=[
+            pltpu.VMEM(pieces, f32),
+            pltpu.VMEM((nf, stored * variables, own_az, radii), f32),
+            pltpu.VMEM((STEPS, variables, own_az, radii), f32),
+            pltpu.VMEM((STEPS, variables, span_az, radii), f32),
+            pltpu.VMEM((2, runs, span_az + 16, radii), f32),
+            pltpu.VMEM((runs, span_az, radii), f32),
+            pltpu.VMEM((rounds, 2, edge_rows, radii), f32),
+            pltpu.VMEM((rounds, 2, edge_rows, radii), f32),
+            pltpu.VMEM((2, own_az + 2, 2 * half, radii), f32),
+            pltpu.VMEM((own_az, 2 * half, radii), f32),
+            pltpu.VMEM((own_az, 2 * half, radii), f32),
+            pltpu.VMEM(((STEPS - 1) * own_az, -(-variables // 8) * 8, radii), f32),
+            pltpu.VMEM(pieces, f32),
+            pltpu.VMEM(pieces, f32),
+            pltpu.SemaphoreType.DMA((4 + STEPS, nf)),
+            pltpu.SemaphoreType.DMA((4 + STEPS, nf)),
+            pltpu.SemaphoreType.DMA((4 + STEPS,)),
+            pltpu.SemaphoreType.DMA((2, SWEEPS + 1)),
+            pltpu.SemaphoreType.DMA((2, SWEEPS + 1)),
+            pltpu.SemaphoreType.DMA((2, rounds)),
+            pltpu.SemaphoreType.DMA((2, rounds)),
+            pltpu.SemaphoreType.DMA((2,)),
+            pltpu.VMEM((freqs, radii), f32),
+            pltpu.VMEM((2 * radii, 2 * radii), jnp.bfloat16),
+            pltpu.VMEM((2 * radii, 2 * radii), jnp.bfloat16),
+            pltpu.VMEM((ntime, 8 * freqs), jnp.bfloat16),
+            pltpu.VMEM((2 * freqs, 4 * ntime), jnp.bfloat16),
+            pltpu.SemaphoreType.DMA((4,)),
+        ],
+        compiler_params=pltpu.CompilerParams(
+            collective_id=0, has_side_effects=True, vmem_limit_bytes=63_000 * 1024
+        ),
+    )(
+        station_index,
+        lobe_count,
+        state_in.reshape(runs, span_az, radii),
+        base_flow.reshape(stored * variables, span_az, radii),
+        forcing_in.reshape(runs, span_az, radii),
+        right_table(inverse_p.T),
+        right_table(slopes.T),
+        left_table(inverse.transpose(2, 0, 1).reshape(ntime, 2 * freqs)),
+        left_table(forward.reshape(2 * freqs, ntime)),
+    )
+    return tuple(y.reshape(state_in.shape) for y in outs)
+
+
+def per_device_any(*args):
+    tiles = args[0].shape[3] % (8 * lax.axis_size("freq")) == 0
+    return (per_device_tiled if tiles else per_device)(*args)
+
+
 MESH = pl.DeviceIdType.MESH
 
 
 def solution(mesh):
     return jax.shard_map(
-        per_device,
+        per_device_any,
         mesh=mesh,
         in_specs=(
             P(None, "freq", None, "plane", None),

time: 157 us -> 156 us (level)
  Pallas kernels: 146 us -> 151 us
  local copies, waits for them, and re-layouts: 6.87 us -> 3.66 us
    pallas_call x1, Pallas kernels: 146 us -> 151 us  [per_device_tiled(): pl.pallas_call(functools.partial(relay, dims), out_shape=[jax.ShapeDtypeS...]
    transpose x2 -> x0, local copies, waits for them, and re-layouts: 3.82 us -> none  [finish(): y.transpose(1, 0, 2, 3).reshape(2, per_dev, variables, nf * own_az, radii)]
    unnamed x2 -> x4, local copies, waits for them, and re-layouts: 0.01 us -> 3.66 us
    reshape x1 -> x0, local copies, waits for them, and re-layouts: 1.72 us -> none  [chunks(): x.reshape(-1, nf, own_az, radii).transpose(1, 0, 2, 3)]
where the time goes in v1:
time: 156 us
  Pallas kernels  151 us (97%)
  local copies, waits for them, and re-layouts  3.66 us (2%)
    pallas_call x1, Pallas kernels, per_device_tiled(): pl.pallas_call(functools.partial(relay, dims), out_shape=[jax.ShapeDtypeS...  151 us
    unnamed x4, local copies, waits for them, and re-layouts  3.66 us

profile of v1, /device:TPU:30, one launch (start us, length us, event | category | flops | bytes accessed | tf_op | source)
XLA Modules:
  0.0 156.2 jit_solution(8258177225830788596)
XLA Ops:
  1.3 151.3 %shard_map.104 = (f32[20,128,128]{2,1,0:T(8,128)}, f32[20,128,128]{2,1,0:T(8,128)}) custom-call(s32[2]{0:T(128)} %station_ref.1, s32[1]{0:T(128)S(6)} %copy.13.lobe_ref, f32[20,128,128]{2,1,0:T(8,128)} %bitcast.5, f32[5,128,128]{2,1,0:T(8,128)} %bitcast.9, f32[20,128,128]{2,1,0:T(8,128)} %bitcast.6, bf16[256,256]{1,0:T(8,128)(2,1)} %constant.8.clone.far_qt, ...), custom_call_target="tpu_custom_call" | custom-call | tf_op jit(solution)/shard_map/pallas_call | solution.py:1095
  152.6 0.0 copy-start
  152.6 2.6 %copy.14 = f32[2,2,5,128,128]{4,3,2,1,0:T(8,128)} copy(f32[2,2,5,128,128]{4,3,2,1,0:T(8,128)} %bitcast.8) | data formatting | bytes 2621440
  155.2 0.0 copy-done
  155.2 1.1 copy.15
Async XLA Ops:
  152.6 2.6 %copy-start = (f32[20,128,128]{2,1,0:T(8,128)S(1)}, f32[20,128,128]{2,1,0:T(8,128)}, u32[]{:S(2)}) copy-start(f32[20,128,128]{2,1,0:T(8,128)} %get-tuple-element.5) | copy-start | bytes 3932164

commit v2 on v1

--- a/solution.py
+++ b/solution.py
@@ -661,9 +661,8 @@
     edge_in,
     x_ref,
     b_ref,
-    f_ref,
     w_ref,
-    o_march,
+    o_state,
     o_forcing,
     send_sem,
     recv_sem,
@@ -683,9 +682,9 @@
     nf, planes, own_az, variables, per_dev, radii, stored = dims
     freqs = nf * per_dev
     span = nf * own_az
-    runs = 2 * per_dev * variables
+    parts = 2 * per_dev
     ntime = inv_ref.shape[0]
-    half = variables * freqs
+    pair = 2 * freqs
     me = lax.axis_index("freq")
     plane = lax.axis_index("plane")
     ring = nf * planes
@@ -711,7 +710,9 @@
 
     beyond = {"freq": me, "plane": (plane + 1) % planes}
     behind = {"freq": me, "plane": (plane + planes - 1) % planes}
-    load_state = pltpu.make_async_copy(state_ref, x_one.at[0, :, pl.ds(8, span), :], load_sem.at[0])
+    load_state = pltpu.make_async_copy(
+        state_ref, x_one.at[0, :, :, pl.ds(8, span), :], load_sem.at[0]
+    )
     load_forcing = pltpu.make_async_copy(forcing_ref, b_one, load_sem.at[1])
     load_state.start()
     load_forcing.start()
@@ -797,110 +798,112 @@
 
     base_start, base_wait = exchange(
         0,
-        lambda i: base_ref.at[:, azimuths(i), :],
+        lambda i: base_ref.at[:, :, azimuths(i), :],
         lambda j: r_base.at[j],
         owner,
         holder,
         me,
     )
-    w_moves = [
-        exchange(
-            1 + s,
-            lambda i, s=s: s_w.at[s],
-            lambda j, s=s: plane_w.at[s, :, azimuths(j), :],
+    groups = [(v, min(v + GROUP, variables)) for v in range(0, variables, GROUP)]
+
+    def w_moves(g):
+        first, stop = groups[g]
+        return exchange(
+            1 + g,
+            lambda i: s_w.at[pl.ds(first, stop - first)],
+            lambda j: plane_w.at[pl.ds(first, stop - first), azimuths(j), :],
             holder,
             owner,
             block,
         )
-        for s in range(STEPS)
-    ]
+
     settled = SWEEPS % 2
-    state_start, state_wait = exchange(
-        1 + STEPS,
-        lambda i: x_one.at[settled, :, pl.ds(pl.multiple_of(8 + i * own_az, 8), own_az), :],
-        lambda j: r_state.at[j],
-        owner,
-        holder,
-        me,
-    )
-    march_start, march_wait = exchange(
-        2 + STEPS,
-        lambda i: o_march.at[i],
-        lambda j: b_one.at[:, azimuths(j), :],
-        holder,
-        owner,
-        block,
-    )
+
+    def state_moves(v):
+        return exchange(
+            1 + variables + v,
+            lambda i: x_one.at[
+                settled, :, v, pl.ds(pl.multiple_of(8 + i * own_az, 8), own_az), :
+            ],
+            lambda j: r_state.at[j, v],
+            owner,
+            holder,
+            me,
+        )
+
+    def out_moves(v):
+        return exchange(
+            1 + 2 * variables + v,
+            lambda i: o_state.at[i, v],
+            lambda j: g_state.at[:, v, azimuths(j), :],
+            holder,
+            owner,
+            block,
+        )
+
     forcing_start, forcing_wait = exchange(
-        3 + STEPS,
+        1 + 3 * variables,
         lambda i: o_forcing.at[i],
-        lambda j: g_forcing.at[:, azimuths(j), :],
+        lambda j: g_forcing.at[:, :, azimuths(j), :],
         holder,
         owner,
         block,
     )
     base_start()
 
-    def halo_copies(e):
+    def halo_copies(e, v):
         slot = e % 2
-        return (
-            pltpu.make_async_remote_copy(
-                src_ref=x_ref.at[slot, own_az],
-                dst_ref=x_ref.at[slot, 0],
-                send_sem=halo_send.at[0, e],
-                recv_sem=halo_recv.at[0, e],
-                device_id=right_id,
-                device_id_type=MESH,
-            ),
-            pltpu.make_async_remote_copy(
-                src_ref=x_ref.at[slot, 1],
-                dst_ref=x_ref.at[slot, own_az + 1],
-                send_sem=halo_send.at[1, e],
-                recv_sem=halo_recv.at[1, e],
-                device_id=left_id,
-                device_id_type=MESH,
-            ),
-        )
-
-    def each_run(visit):
-        @pl.loop(0, own_az)
-        def _(a):
-            for c in range(2):
-                for v in range(variables):
-                    for kk in range(per_dev):
-                        start = ((c * variables + v) * per_dev + kk) * nf
-                        visit(a, start, (c * per_dev + kk) * variables + v)
-
-    def edge_copies(e):
+        rows = pl.ds(pl.multiple_of(v * pair, 8), pair)
         return [
             pltpu.make_async_remote_copy(
-                src_ref=edge_out.at[e, side],
-                dst_ref=edge_in.at[e, side],
-                send_sem=edge_send.at[side, e],
-                recv_sem=edge_recv.at[side, e],
+                src_ref=x_ref.at[slot, source, rows, :],
+                dst_ref=x_ref.at[slot, target, rows, :],
+                send_sem=halo_send.at[side, e, v],
+                recv_sem=halo_recv.at[side, e, v],
+                device_id=device,
+                device_id_type=MESH,
+            )
+            for side, source, target, device in (
+                (0, own_az, 0, right_id),
+                (1, 1, own_az + 1, left_id),
+            )
+        ]
+
+    def edge_copies(e, v):
+        return [
+            pltpu.make_async_remote_copy(
+                src_ref=edge_out.at[e, v, side],
+                dst_ref=edge_in.at[e, v, side],
+                send_sem=edge_send.at[side, e, v],
+                recv_sem=edge_recv.at[side, e, v],
                 device_id=target,
                 device_id_type=MESH,
             )
             for side, target in ((0, beyond), (1, behind))
         ]
 
-    def send_edges(slot, e):
-        for m in range(runs):
-            edge_out[e, 0, pl.ds(m, 1), :] = x_one[slot, m, pl.ds(7 + span, 1), :]
-            edge_out[e, 1, pl.ds(m, 1), :] = x_one[slot, m, pl.ds(8, 1), :]
-        for copy in edge_copies(e):
+    def send_edges(slot, e, v):
+        for ck in range(parts):
+            edge_out[e, v, 0, pl.ds(ck, 1), :] = x_one[slot, ck, v, pl.ds(7 + span, 1), :]
+            edge_out[e, v, 1, pl.ds(ck, 1), :] = x_one[slot, ck, v, pl.ds(8, 1), :]
+        for copy in edge_copies(e, v):
             copy.start()
 
     for kk in range(per_dev):
         modes = lax.broadcasted_iota(jnp.int32, (nf, radii), 0) * per_dev + kk
         omega_ref[pl.ds(kk * nf, nf), :] = 0.5 * modes.astype(jnp.float32) / freqs
     load_state.wait()
-    send_edges(0, 0)
+
+    @pl.loop(0, variables)
+    def _(v):
+        send_edges(0, 0, v)
+
     load_forcing.wait()
 
-    @pl.loop(0, runs)
-    def _(m):
-        b_one[m] = MARCH_WEIGHT * x_one[0, m, pl.ds(8, span), :] + b_one[m]
+    @pl.loop(0, variables)
+    def _(v):
+        for ck in range(parts):
+            b_one[ck, v] = MARCH_WEIGHT * x_one[0, ck, v, pl.ds(8, span), :] + b_one[ck, v]
 
     for table in tables:
         table.wait()
@@ -908,91 +911,99 @@
     phases = (lobe_ref[0] * position) % (span * planes)
     shape = 1.0 + 0.5 * jnp.cos(2.0 * math.pi * phases.astype(jnp.float32) / (span * planes))
     base_wait()
-    for station in range(STEPS):
+
+    def coefficient(station, v):
         wanted = station_ref[station]
-        for v in range(variables):
-            scaled = (BASE_SCALE * shape) * r_base[
-                wanted // stored, (wanted % stored) * variables + v
-            ]
-            s_w[station, v] = scaled
-            if station > 0:
-                for a in range(own_az):
-                    w_ref[(station - 1) * own_az + a, pl.ds(v, 1), :] = scaled[a : a + 1]
-        w_moves[station][0]()
-
-    def freq_sweeps(station):
-        @pl.loop(0, SWEEPS)
-        def _(sweep):
-            e = station * SWEEPS + sweep
+        return (BASE_SCALE * shape) * r_base[wanted // stored, wanted % stored, v]
+
+    for g, (first, stop) in enumerate(groups):
+        for v in range(first, stop):
+            s_w[v] = coefficient(0, v)
+        w_moves(g)[0]()
+    for v in range(variables):
+        w_ref[v] = coefficient(1, v)
+
+    for g, (first, stop) in enumerate(groups):
+        w_moves(g)[1]()
+
+        @pl.loop(0, SWEEPS * (stop - first))
+        def _(turn):
+            e, v = turn // (stop - first), first + turn % (stop - first)
             src, dst = e % 2, (e + 1) % 2
-            for copy in edge_copies(e):
+            for copy in edge_copies(e, v):
                 copy.wait()
-            for m in range(runs):
-                x_one[src, m, pl.ds(7, 1), :] = edge_in[e, 0, pl.ds(m, 1), :]
-                x_one[src, m, pl.ds(8 + span, 1), :] = edge_in[e, 1, pl.ds(m, 1), :]
+            for ck in range(parts):
+                x_one[src, ck, v, pl.ds(7, 1), :] = edge_in[e, v, 0, pl.ds(ck, 1), :]
+                x_one[src, ck, v, pl.ds(8 + span, 1), :] = edge_in[e, v, 1, pl.ds(ck, 1), :]
+            w = plane_w[v]
             for kk in range(per_dev):
                 rate = (me * per_dev + kk).astype(jnp.float32) * (0.5 / freqs)
-
-                @pl.loop(0, variables)
-                def _(v):
-                    w = plane_w[station, v]
-                    at = [(c * per_dev + kk) * variables + v for c in range(2)]
-                    real, imag = [x_one[src, m, pl.ds(8, span), :] for m in at]
-                    mixing = (w * real - rate * imag, w * imag + rate * real)
-                    summed = [
-                        SIDE_WEIGHT
-                        * (x_one[src, m, pl.ds(7, span), :] + x_one[src, m, pl.ds(9, span), :])
-                        + b_one[m]
-                        - mixed
-                        for m, mixed in zip(at, mixing)
-                    ]
-                    q = times_right(jnp.concatenate(summed, axis=0), qt_ref[...])
-                    x_one[dst, at[0], pl.ds(8, span), :] = q[:span]
-                    x_one[dst, at[1], pl.ds(8, span), :] = q[span:]
-
-            @pl.when(e < STEPS * SWEEPS - 1)
+                at = [c * per_dev + kk for c in range(2)]
+                real, imag = [x_one[src, ck, v, pl.ds(8, span), :] for ck in at]
+                mixing = (w * real - rate * imag, w * imag + rate * real)
+                summed = [
+                    SIDE_WEIGHT
+                    * (x_one[src, ck, v, pl.ds(7, span), :] + x_one[src, ck, v, pl.ds(9, span), :])
+                    + b_one[ck, v]
+                    - mixed
+                    for ck, mixed in zip(at, mixing)
+                ]
+                q = times_right(jnp.concatenate(summed, axis=0), qt_ref[...])
+                x_one[dst, at[0], v, pl.ds(8, span), :] = q[:span]
+                x_one[dst, at[1], v, pl.ds(8, span), :] = q[span:]
+
+            @pl.when(e < SWEEPS - 1)
             def _():
-                send_edges(dst, e + 1)
-
-    w_moves[0][1]()
-    freq_sweeps(0)
-    state_start()
-    state_wait()
-
-    def unpack_state(a, start, m):
-        x_ref[0, a + 1, pl.ds(start, nf), :] = r_state[:, m, a, :]
-
-    each_run(unpack_state)
-    for copy in halo_copies(0):
-        copy.start()
-    omega = omega_ref[...][None]
-    flat = (2 * half, radii)
-    cube = (variables, freqs, radii)
-
-    def sweep_slab(src, dst, a, station):
-        x = x_ref[src, a + 1]
-        beside = SIDE_WEIGHT * (x_ref[src, a] + x_ref[src, a + 2]) + b_ref[a]
-        real, imag = x[:half].reshape(cube), x[half:].reshape(cube)
-        w = w_ref[(station - 1) * own_az + a][:variables][:, None, :]
-        mixing = jnp.concatenate([w * real - omega * imag, w * imag + omega * real], axis=0)
-        summed = beside - mixing.reshape(flat)
-        x_ref[dst, a + 1] = times_right(summed, qt_ref[...])
+                send_edges(dst, e + 1, v)
+
+            @pl.when(e == SWEEPS - 1)
+            def _():
+                state_moves(v)[0]()
+
+    def each_run(v, visit):
+        for c in range(2):
+            for kk in range(per_dev):
+                start = pl.multiple_of(v * pair + (c * per_dev + kk) * nf, 8)
+                visit(start, c * per_dev + kk)
+
+    @pl.loop(0, variables)
+    def _(v):
+        state_moves(v)[1]()
+
+        @pl.loop(0, own_az)
+        def _(a):
+            def unpack(start, ck):
+                x_ref[0, a + 1, pl.ds(start, nf), :] = r_state[:, v, ck, a, :]
+
+            each_run(v, unpack)
+
+        for copy in halo_copies(0, v):
+            copy.start()
+
+    omega = omega_ref[...]
+
+    def sweep_slabs(e, v):
+        src, dst = e % 2, (e + 1) % 2
+        rows = pl.ds(pl.multiple_of(v * pair, 8), pair)
+        w = w_ref[v]
+        summed = []
+        for a in range(own_az):
+            x = x_ref[src, a + 1, rows, :]
+            beside = SIDE_WEIGHT * (x_ref[src, a, rows, :] + x_ref[src, a + 2, rows, :])
+            real, imag = x[:freqs], x[freqs:]
+            here_w = w[a : a + 1]
+            mixing = [here_w * real - omega * imag, here_w * imag + omega * real]
+            summed.append(beside + b_ref[a, rows, :] - jnp.concatenate(mixing, axis=0))
+        q = times_right(jnp.concatenate(summed, axis=0), qt_ref[...])
+        for a in range(own_az):
+            x_ref[dst, a + 1, rows, :] = q[a * pair : (a + 1) * pair]
 
     def advect_slab(slot, a, final):
         x = x_ref[slot, a + 1]
         beside = 0.5 * (x_ref[slot, a + 2] - x_ref[slot, a])
 
         def lanes(y):
-            return [
-                jnp.concatenate(
-                    [
-                        y[v * freqs : (v + 1) * freqs],
-                        y[half + v * freqs : half + (v + 1) * freqs],
-                    ],
-                    axis=0,
-                )
-                for v in range(variables)
-            ]
+            return [y[v * pair : (v + 1) * pair] for v in range(variables)]
 
         both = jnp.concatenate(lanes(x) + lanes(beside), axis=1)
         in_time = times_left(inv_ref[...], both)
@@ -1007,69 +1018,69 @@
         n[0] = n[0] + u[0] * (ur[1] + ua[2])
         source = -ADVECT_SCALE * jnp.concatenate(n, axis=1)
         spectral = times_left(fwd_ref[...], source)
-        forcing = jnp.concatenate(
-            [
-                spectral[c * freqs : (c + 1) * freqs, v * radii : (v + 1) * radii]
-                for c in range(2)
-                for v in range(variables)
-            ],
-            axis=0,
-        )
-        if final:
-            f_ref[a] = forcing
-        else:
-            b_ref[a] = MARCH_WEIGHT * x + forcing
-
-    def advect_all(slot, e, final):
+        for v in range(variables):
+            forcing = spectral[:, v * radii : (v + 1) * radii]
+            if final:
+                for ck in range(parts):
+                    o_forcing[:, ck, v, a, :] = forcing[ck * nf : (ck + 1) * nf]
+            else:
+                b_ref[a, pl.ds(v * pair, pair), :] = (
+                    MARCH_WEIGHT * x[v * pair : (v + 1) * pair] + forcing
+                )
+
+    def advect_all(e, final):
+        slot = e % 2
+
         @pl.loop(1, own_az - 1)
         def _(a):
             advect_slab(slot, a, final)
 
-        for copy in halo_copies(e):
-            copy.wait()
-        advect_slab(slot, 0, final)
-        advect_slab(slot, own_az - 1, final)
-
-    def pack_march(a, start, m):
-        o_march[:, m, a, :] = b_ref[a, pl.ds(start, nf), :]
-
-    def pack_forcing(a, start, m):
-        o_forcing[:, m, a, :] = f_ref[a, pl.ds(start, nf), :]
-
-    advect_all(0, 0, False)
-    each_run(pack_march)
-    march_start()
-
-    @pl.loop(0, SWEEPS)
-    def _(e):
-        src, dst = e % 2, (e + 1) % 2
+        @pl.loop(0, variables)
+        def _(v):
+            for copy in halo_copies(e, v):
+                copy.wait()
+
+        @pl.loop(0, 2)
+        def _(side):
+            advect_slab(slot, side * (own_az - 1), final)
+
+    advect_all(0, False)
+
+    @pl.loop(0, SWEEPS * variables)
+    def _(turn):
+        e, v = turn // variables, turn % variables
 
         @pl.when(e > 0)
         def _():
-            for copy in halo_copies(e):
+            for copy in halo_copies(e, v):
                 copy.wait()
 
-        sweep_slab(src, dst, 0, 1)
-        sweep_slab(src, dst, own_az - 1, 1)
-        for copy in halo_copies(e + 1):
+        sweep_slabs(e, v)
+        for copy in halo_copies(e + 1, v):
             copy.start()
 
-        @pl.loop(1, own_az - 1)
-        def _(a):
-            sweep_slab(src, dst, a, 1)
-
-    advect_all(SWEEPS % 2, SWEEPS, True)
-    each_run(pack_forcing)
-    march_wait()
+        @pl.when(e == SWEEPS - 1)
+        def _():
+            @pl.loop(0, own_az)
+            def _(a):
+                def pack(start, ck):
+                    o_state[:, v, ck, a, :] = x_ref[settled, a + 1, pl.ds(start, nf), :]
+
+                each_run(v, pack)
+
+            out_moves(v)[0]()
+
+    advect_all(SWEEPS, True)
     forcing_start()
-    w_moves[1][1]()
-    freq_sweeps(1)
-    out_state = pltpu.make_async_copy(
-        x_one.at[(2 * SWEEPS) % 2, :, pl.ds(8, span), :], g_state, load_sem.at[0]
-    )
-    out_state.start()
-    out_state.wait()
+
+    @pl.loop(0, variables)
+    def _(v):
+        out_moves(v)[1]()
+
     forcing_wait()
+
+
+GROUP = 3
 
 
 def per_device_tiled(state_in, forcing_in, base_flow, station_index, lobe_count):
@@ -1084,41 +1095,40 @@
     mode_ids = (np.arange(nf)[None, :] * per_dev + np.arange(per_dev)[:, None]).reshape(-1)
     inverse, forward = transform_tables(mode_ids, freqs, ntime)
     dims = (nf, planes, own_az, variables, per_dev, radii, stored)
-    half = variables * freqs
-    runs = 2 * per_dev * variables
-    edge_rows = -(-runs // 8) * 8
-    rounds = STEPS * SWEEPS
+    parts = 2 * per_dev
+    edge_rows = -(-parts // 8) * 8
     smem = pl.BlockSpec(memory_space=pltpu.SMEM)
     anywhere = pl.BlockSpec(memory_space=pl.ANY)
     f32 = jnp.float32
-    pieces = (nf, runs, own_az, radii)
+    whole = (parts, variables, span_az, radii)
+    slab = variables * 2 * freqs
+    moves = 2 + 3 * variables
     outs = pl.pallas_call(
         functools.partial(relay, dims),
-        out_shape=[jax.ShapeDtypeStruct((runs, span_az, radii), f32)] * 2,
+        out_shape=[jax.ShapeDtypeStruct(whole, f32)] * 2,
         in_specs=[smem, smem] + [anywhere] * 7,
         out_specs=[anywhere, anywhere],
         scratch_shapes=[
-            pltpu.VMEM(pieces, f32),
-            pltpu.VMEM((nf, stored * variables, own_az, radii), f32),
-            pltpu.VMEM((STEPS, variables, own_az, radii), f32),
-            pltpu.VMEM((STEPS, variables, span_az, radii), f32),
-            pltpu.VMEM((2, runs, span_az + 16, radii), f32),
-            pltpu.VMEM((runs, span_az, radii), f32),
-            pltpu.VMEM((rounds, 2, edge_rows, radii), f32),
-            pltpu.VMEM((rounds, 2, edge_rows, radii), f32),
-            pltpu.VMEM((2, own_az + 2, 2 * half, radii), f32),
-            pltpu.VMEM((own_az, 2 * half, radii), f32),
-            pltpu.VMEM((own_az, 2 * half, radii), f32),
-            pltpu.VMEM(((STEPS - 1) * own_az, -(-variables // 8) * 8, radii), f32),
-            pltpu.VMEM(pieces, f32),
-            pltpu.VMEM(pieces, f32),
-            pltpu.SemaphoreType.DMA((4 + STEPS, nf)),
-            pltpu.SemaphoreType.DMA((4 + STEPS, nf)),
-            pltpu.SemaphoreType.DMA((4 + STEPS,)),
-            pltpu.SemaphoreType.DMA((2, SWEEPS + 1)),
-            pltpu.SemaphoreType.DMA((2, SWEEPS + 1)),
-            pltpu.SemaphoreType.DMA((2, rounds)),
-            pltpu.SemaphoreType.DMA((2, rounds)),
+            pltpu.VMEM((nf, variables, parts, own_az, radii), f32),
+            pltpu.VMEM((nf, stored, variables, own_az, radii), f32),
+            pltpu.VMEM((variables, own_az, radii), f32),
+            pltpu.VMEM((variables, span_az, radii), f32),
+            pltpu.VMEM((2, parts, variables, span_az + 16, radii), f32),
+            pltpu.VMEM(whole, f32),
+            pltpu.VMEM((SWEEPS, variables, 2, edge_rows, radii), f32),
+            pltpu.VMEM((SWEEPS, variables, 2, edge_rows, radii), f32),
+            pltpu.VMEM((2, own_az + 2, slab, radii), f32),
+            pltpu.VMEM((own_az, slab, radii), f32),
+            pltpu.VMEM((variables, own_az, radii), f32),
+            pltpu.VMEM((nf, variables, parts, own_az, radii), f32),
+            pltpu.VMEM((nf, parts, variables, own_az, radii), f32),
+            pltpu.SemaphoreType.DMA((moves, nf)),
+            pltpu.SemaphoreType.DMA((moves, nf)),
+            pltpu.SemaphoreType.DMA((moves,)),
+            pltpu.SemaphoreType.DMA((2, SWEEPS + 1, variables)),
+            pltpu.SemaphoreType.DMA((2, SWEEPS + 1, variables)),
+            pltpu.SemaphoreType.DMA((2, SWEEPS, variables)),
+            pltpu.SemaphoreType.DMA((2, SWEEPS, variables)),
             pltpu.SemaphoreType.DMA((2,)),
             pltpu.VMEM((freqs, radii), f32),
             pltpu.VMEM((2 * radii, 2 * radii), jnp.bfloat16),
@@ -1133,9 +1143,9 @@
     )(
         station_index,
         lobe_count,
-        state_in.reshape(runs, span_az, radii),
-        base_flow.reshape(stored * variables, span_az, radii),
-        forcing_in.reshape(runs, span_az, radii),
+        state_in.reshape(whole),
+        base_flow,
+        forcing_in.reshape(whole),
         right_table(inverse_p.T),
         right_table(slopes.T),
         left_table(inverse.transpose(2, 0, 1).reshape(ntime, 2 * freqs)),

time: 156 us -> 144 us (0.923); the launches traced: 156 us -> 142 us
  Pallas kernels: 151 us -> 137 us
    pallas_call x1, Pallas kernels: 151 us -> 137 us  [per_device_tiled(): pl.pallas_call(functools.partial(relay, dims), out_shape=[jax.ShapeDtypeS...]
where the time goes in v2:
time: 144 us; the launch traced here: 142 us
  Pallas kernels  137 us (95%)
  local copies, waits for them, and re-layouts  3.66 us (3%)
    pallas_call x1, Pallas kernels, per_device_tiled(): pl.pallas_call(functools.partial(relay, dims), out_shape=[jax.ShapeDtypeS...  137 us
    unnamed x4, local copies, waits for them, and re-layouts  3.66 us

profile of v2, /device:TPU:30, one launch (start us, length us, event | category | flops | bytes accessed | tf_op | source)
XLA Modules:
  0.0 142.0 jit_solution(2489730308924571424)
XLA Ops:
  1.3 137.1 %shard_map.104 = (f32[4,5,128,128]{3,2,1,0:T(8,128)}, f32[4,5,128,128]{3,2,1,0:T(8,128)}) custom-call(s32[2]{0:T(128)} %station_ref.1, s32[1]{0:T(128)S(6)} %copy.13.lobe_ref, f32[4,5,128,128]{3,2,1,0:T(8,128)} %bitcast.4, f32[1,5,128,128]{3,2,1,0:T(8,128)} %base_ref.1, f32[4,5,128,128]{3,2,1,0:T(8,128)} %bitcast.5, bf16[256,256]{1,0:T(8,128)(2,1)} %constant.8.clone.far_qt, ...), custom_call_target="tpu_custom_call" | custom-call | tf_op jit(solution)/shard_map/pallas_call | solution.py:1106
  138.4 0.0 copy-start
  138.4 2.6 %copy.14 = f32[2,2,5,128,128]{4,3,2,1,0:T(8,128)} copy(f32[2,2,5,128,128]{4,3,2,1,0:T(8,128)} %bitcast.7) | data formatting | bytes 2621440
  141.0 0.0 copy-done
  141.0 1.1 copy.15
Async XLA Ops:
  138.4 2.6 %copy-start = (f32[4,5,128,128]{3,2,1,0:T(8,128)S(1)}, f32[4,5,128,128]{3,2,1,0:T(8,128)}, u32[]{:S(2)}) copy-start(f32[4,5,128,128]{3,2,1,0:T(8,128)} %get-tuple-element.5) | copy-start | bytes 3932164

commit v3 on v2

--- a/solution.py
+++ b/solution.py
@@ -638,10 +638,21 @@
     return y.transpose(1, 0, 2, 3).reshape(2, per_dev, variables, nf * own_az, radii)
 
 
+def stacked_table(table):
+    high, low = np_halves(table)
+    return jnp.asarray(np.tile(np.concatenate([high, low], axis=0), (1, 2)))
+
+
+def times_stacked(table, x):
+    height = table.shape[0] // 2
+    y = jnp.dot(table, jnp.concatenate(halves(x), axis=0), preferred_element_type=jnp.float32)
+    return y[:height] + y[height:]
+
+
 def relay(
     dims,
-    station_ref,
     lobe_ref,
+    far_station,
     state_ref,
     base_ref,
     forcing_ref,
@@ -663,6 +674,7 @@
     b_ref,
     w_ref,
     o_state,
+    o_march,
     o_forcing,
     send_sem,
     recv_sem,
@@ -678,12 +690,13 @@
     inv_ref,
     fwd_ref,
     table_sem,
+    station_ref,
 ):
     nf, planes, own_az, variables, per_dev, radii, stored = dims
     freqs = nf * per_dev
     span = nf * own_az
     parts = 2 * per_dev
-    ntime = inv_ref.shape[0]
+    ntime = inv_ref.shape[0] // 2
     pair = 2 * freqs
     me = lax.axis_index("freq")
     plane = lax.axis_index("plane")
@@ -694,22 +707,28 @@
     def named(device):
         return {"freq": device[0], "plane": device[1]}
 
+    def is_me(device):
+        return (device[0] == me) & (device[1] == plane)
+
     right_id = named(device_of((here + 1) % ring, nf, planes))
     left_id = named(device_of((here + ring - 1) % ring, nf, planes))
     barrier = pltpu.get_barrier_semaphore()
 
-    @pl.loop(1, ring)
+    def greet(device):
+        pl.semaphore_signal(barrier, inc=1, device_id=device, device_id_type=MESH)
+
+    @pl.loop(0, nf)
     def _(d):
-        other = (me * planes + plane + d) % ring
-        pl.semaphore_signal(
-            barrier,
-            inc=1,
-            device_id={"freq": other // planes, "plane": other % planes},
-            device_id_type=MESH,
-        )
+        i = (me + nf // 2 + d) % nf
+
+        @pl.when(jnp.logical_not(is_me((i, part))))
+        def _():
+            greet(named((i, part)))
 
     beyond = {"freq": me, "plane": (plane + 1) % planes}
     behind = {"freq": me, "plane": (plane + planes - 1) % planes}
+    for device in (beyond, right_id, left_id):
+        greet(device)
     load_state = pltpu.make_async_copy(
         state_ref, x_one.at[0, :, :, pl.ds(8, span), :], load_sem.at[0]
     )
@@ -719,12 +738,18 @@
     tables = [
         pltpu.make_async_copy(far, near, table_sem.at[i])
         for i, (far, near) in enumerate(
-            ((far_qt, qt_ref), (far_st, st_ref), (far_inv, inv_ref), (far_fwd, fwd_ref))
+            (
+                (far_station, station_ref),
+                (far_qt, qt_ref),
+                (far_st, st_ref),
+                (far_inv, inv_ref),
+                (far_fwd, fwd_ref),
+            )
         )
     ]
     for table in tables:
         table.start()
-    pl.semaphore_wait(barrier, ring - 1)
+    pl.semaphore_wait(barrier, nf + 3 - (part == plane).astype(jnp.int32))
 
     def owner(i):
         return device_of(plane * nf + i, nf, planes)
@@ -732,11 +757,11 @@
     def holder(i):
         return i, part
 
-    def is_me(device):
-        return (device[0] == me) & (device[1] == plane)
-
     def azimuths(i):
         return pl.ds(pl.multiple_of(i * own_az, 8), own_az)
+
+    def mixed(d):
+        return d
 
     def exchange(k, piece, landing, target, origin, mine):
         def copy(i):
@@ -762,10 +787,10 @@
         def own(i):
             return pltpu.make_async_copy(piece(i), landing(mine), own_sem.at[k])
 
-        def start():
-            @pl.loop(0, nf)
+        def start(first=0, stop=nf):
+            @pl.loop(first, stop)
             def _(d):
-                i = (d + me) % nf
+                i = (mixed(d) + me) % nf
                 stays = is_me(target(i))
 
                 @pl.when(stays)
@@ -810,8 +835,27 @@
         first, stop = groups[g]
         return exchange(
             1 + g,
-            lambda i: s_w.at[pl.ds(first, stop - first)],
-            lambda j: plane_w.at[pl.ds(first, stop - first), azimuths(j), :],
+            lambda i: s_w.at[0, pl.ds(first, stop - first)],
+            lambda j: plane_w.at[0, pl.ds(first, stop - first), azimuths(j), :],
+            holder,
+            owner,
+            block,
+        )
+
+    later_start, later_wait = exchange(
+        2 + 3 * variables,
+        lambda i: s_w.at[1, pl.ds(0, RETURNED)],
+        lambda j: plane_w.at[1, pl.ds(0, RETURNED), azimuths(j), :],
+        holder,
+        owner,
+        block,
+    )
+
+    def march_moves(v):
+        return exchange(
+            3 + 3 * variables + v,
+            lambda i: o_march.at[i, v],
+            lambda j: b_one.at[:, v, azimuths(j), :],
             holder,
             owner,
             block,
@@ -918,10 +962,36 @@
 
     for g, (first, stop) in enumerate(groups):
         for v in range(first, stop):
-            s_w[v] = coefficient(0, v)
+            s_w[0, v] = coefficient(0, v)
         w_moves(g)[0]()
     for v in range(variables):
         w_ref[v] = coefficient(1, v)
+        if v < RETURNED:
+            s_w[1, v] = coefficient(1, v)
+    later_start()
+
+    def sweep_plane(e, v, w):
+        src, dst = e % 2, (e + 1) % 2
+        for copy in edge_copies(e, v):
+            copy.wait()
+        for ck in range(parts):
+            x_one[src, ck, v, pl.ds(7, 1), :] = edge_in[e, v, 0, pl.ds(ck, 1), :]
+            x_one[src, ck, v, pl.ds(8 + span, 1), :] = edge_in[e, v, 1, pl.ds(ck, 1), :]
+        for kk in range(per_dev):
+            rate = (me * per_dev + kk).astype(jnp.float32) * (0.5 / freqs)
+            at = [c * per_dev + kk for c in range(2)]
+            real, imag = [x_one[src, ck, v, pl.ds(8, span), :] for ck in at]
+            mixing = (w * real - rate * imag, w * imag + rate * real)
+            summed = [
+                SIDE_WEIGHT
+                * (x_one[src, ck, v, pl.ds(7, span), :] + x_one[src, ck, v, pl.ds(9, span), :])
+                + b_one[ck, v]
+                - mixed_in
+                for ck, mixed_in in zip(at, mixing)
+            ]
+            q = times_right(jnp.concatenate(summed, axis=0), qt_ref[...])
+            x_one[dst, at[0], v, pl.ds(8, span), :] = q[:span]
+            x_one[dst, at[1], v, pl.ds(8, span), :] = q[span:]
 
     for g, (first, stop) in enumerate(groups):
         w_moves(g)[1]()
@@ -929,32 +999,11 @@
         @pl.loop(0, SWEEPS * (stop - first))
         def _(turn):
             e, v = turn // (stop - first), first + turn % (stop - first)
-            src, dst = e % 2, (e + 1) % 2
-            for copy in edge_copies(e, v):
-                copy.wait()
-            for ck in range(parts):
-                x_one[src, ck, v, pl.ds(7, 1), :] = edge_in[e, v, 0, pl.ds(ck, 1), :]
-                x_one[src, ck, v, pl.ds(8 + span, 1), :] = edge_in[e, v, 1, pl.ds(ck, 1), :]
-            w = plane_w[v]
-            for kk in range(per_dev):
-                rate = (me * per_dev + kk).astype(jnp.float32) * (0.5 / freqs)
-                at = [c * per_dev + kk for c in range(2)]
-                real, imag = [x_one[src, ck, v, pl.ds(8, span), :] for ck in at]
-                mixing = (w * real - rate * imag, w * imag + rate * real)
-                summed = [
-                    SIDE_WEIGHT
-                    * (x_one[src, ck, v, pl.ds(7, span), :] + x_one[src, ck, v, pl.ds(9, span), :])
-                    + b_one[ck, v]
-                    - mixed
-                    for ck, mixed in zip(at, mixing)
-                ]
-                q = times_right(jnp.concatenate(summed, axis=0), qt_ref[...])
-                x_one[dst, at[0], v, pl.ds(8, span), :] = q[:span]
-                x_one[dst, at[1], v, pl.ds(8, span), :] = q[span:]
-
-            @pl.when(e < SWEEPS - 1)
+            sweep_plane(e, v, plane_w[0, v])
+
+            @pl.when((e < SWEEPS - 1) | (v < RETURNED))
             def _():
-                send_edges(dst, e + 1, v)
+                send_edges((e + 1) % 2, e + 1, v)
 
             @pl.when(e == SWEEPS - 1)
             def _():
@@ -1006,7 +1055,7 @@
             return [y[v * pair : (v + 1) * pair] for v in range(variables)]
 
         both = jnp.concatenate(lanes(x) + lanes(beside), axis=1)
-        in_time = times_left(inv_ref[...], both)
+        in_time = times_stacked(inv_ref[...], both)
         u = [in_time[:, v * radii : (v + 1) * radii] for v in range(variables)]
         ua = [
             in_time[:, (variables + v) * radii : (variables + v + 1) * radii]
@@ -1017,16 +1066,18 @@
         n = [u[1] * ur[v] + u[2] * ua[v] for v in range(variables)]
         n[0] = n[0] + u[0] * (ur[1] + ua[2])
         source = -ADVECT_SCALE * jnp.concatenate(n, axis=1)
-        spectral = times_left(fwd_ref[...], source)
+        spectral = times_stacked(fwd_ref[...], source)
         for v in range(variables):
             forcing = spectral[:, v * radii : (v + 1) * radii]
             if final:
                 for ck in range(parts):
                     o_forcing[:, ck, v, a, :] = forcing[ck * nf : (ck + 1) * nf]
             else:
-                b_ref[a, pl.ds(v * pair, pair), :] = (
-                    MARCH_WEIGHT * x[v * pair : (v + 1) * pair] + forcing
-                )
+                march = MARCH_WEIGHT * x[v * pair : (v + 1) * pair] + forcing
+                b_ref[a, pl.ds(v * pair, pair), :] = march
+                if v < RETURNED:
+                    for ck in range(parts):
+                        o_march[:, v, ck, a, :] = march[ck * nf : (ck + 1) * nf]
 
     def advect_all(e, final):
         slot = e % 2
@@ -1059,7 +1110,12 @@
         for copy in halo_copies(e + 1, v):
             copy.start()
 
-        @pl.when(e == SWEEPS - 1)
+        @pl.when(turn < nf)
+        def _():
+            for w in range(RETURNED):
+                march_moves(w)[0](turn, turn + 1)
+
+        @pl.when((e == SWEEPS - 1) & (v >= RETURNED))
         def _():
             @pl.loop(0, own_az)
             def _(a):
@@ -1072,15 +1128,37 @@
 
     advect_all(SWEEPS, True)
     forcing_start()
-
-    @pl.loop(0, variables)
+    later_wait()
+    for v in range(RETURNED):
+        march_moves(v)[1]()
+
+    @pl.loop(0, SWEEPS * RETURNED)
+    def _(turn):
+        e, v = SWEEPS + turn // RETURNED, turn % RETURNED
+        sweep_plane(e, v, plane_w[1, v])
+
+        @pl.when(e < 2 * SWEEPS - 1)
+        def _():
+            send_edges((e + 1) % 2, e + 1, v)
+
+    out_state = pltpu.make_async_copy(
+        x_one.at[0, :, pl.ds(0, RETURNED), pl.ds(8, span), :],
+        g_state.at[:, pl.ds(0, RETURNED), :, :],
+        load_sem.at[0],
+    )
+    out_state.start()
+
+    @pl.loop(RETURNED, variables)
     def _(v):
         out_moves(v)[1]()
 
+    out_state.wait()
+
     forcing_wait()
 
 
-GROUP = 3
+GROUP = 1
+RETURNED = 1
 
 
 def per_device_tiled(state_in, forcing_in, base_flow, station_index, lobe_count):
@@ -1097,59 +1175,67 @@
     dims = (nf, planes, own_az, variables, per_dev, radii, stored)
     parts = 2 * per_dev
     edge_rows = -(-parts // 8) * 8
-    smem = pl.BlockSpec(memory_space=pltpu.SMEM)
     anywhere = pl.BlockSpec(memory_space=pl.ANY)
+    far = pl.BlockSpec(memory_space=pltpu.HBM)
     f32 = jnp.float32
     whole = (parts, variables, span_az, radii)
     slab = variables * 2 * freqs
-    moves = 2 + 3 * variables
+    moves = 3 + 3 * variables + RETURNED
+    rounds = 2 * SWEEPS
     outs = pl.pallas_call(
         functools.partial(relay, dims),
         out_shape=[jax.ShapeDtypeStruct(whole, f32)] * 2,
-        in_specs=[smem, smem] + [anywhere] * 7,
+        in_specs=[pl.BlockSpec(memory_space=pltpu.SMEM)] + [far] * 8,
         out_specs=[anywhere, anywhere],
         scratch_shapes=[
             pltpu.VMEM((nf, variables, parts, own_az, radii), f32),
             pltpu.VMEM((nf, stored, variables, own_az, radii), f32),
-            pltpu.VMEM((variables, own_az, radii), f32),
-            pltpu.VMEM((variables, span_az, radii), f32),
+            pltpu.VMEM((2, variables, own_az, radii), f32),
+            pltpu.VMEM((2, variables, span_az, radii), f32),
             pltpu.VMEM((2, parts, variables, span_az + 16, radii), f32),
             pltpu.VMEM(whole, f32),
-            pltpu.VMEM((SWEEPS, variables, 2, edge_rows, radii), f32),
-            pltpu.VMEM((SWEEPS, variables, 2, edge_rows, radii), f32),
+            pltpu.VMEM((rounds, variables, 2, edge_rows, radii), f32),
+            pltpu.VMEM((rounds, variables, 2, edge_rows, radii), f32),
             pltpu.VMEM((2, own_az + 2, slab, radii), f32),
             pltpu.VMEM((own_az, slab, radii), f32),
             pltpu.VMEM((variables, own_az, radii), f32),
             pltpu.VMEM((nf, variables, parts, own_az, radii), f32),
+            pltpu.VMEM((nf, RETURNED, parts, own_az, radii), f32),
             pltpu.VMEM((nf, parts, variables, own_az, radii), f32),
             pltpu.SemaphoreType.DMA((moves, nf)),
             pltpu.SemaphoreType.DMA((moves, nf)),
             pltpu.SemaphoreType.DMA((moves,)),
             pltpu.SemaphoreType.DMA((2, SWEEPS + 1, variables)),
             pltpu.SemaphoreType.DMA((2, SWEEPS + 1, variables)),
-            pltpu.SemaphoreType.DMA((2, SWEEPS, variables)),
-            pltpu.SemaphoreType.DMA((2, SWEEPS, variables)),
+            pltpu.SemaphoreType.DMA((2, rounds, variables)),
+            pltpu.SemaphoreType.DMA((2, rounds, variables)),
             pltpu.SemaphoreType.DMA((2,)),
             pltpu.VMEM((freqs, radii), f32),
             pltpu.VMEM((2 * radii, 2 * radii), jnp.bfloat16),
             pltpu.VMEM((2 * radii, 2 * radii), jnp.bfloat16),
-            pltpu.VMEM((ntime, 8 * freqs), jnp.bfloat16),
-            pltpu.VMEM((2 * freqs, 4 * ntime), jnp.bfloat16),
-            pltpu.SemaphoreType.DMA((4,)),
+            pltpu.VMEM((2 * ntime, 4 * freqs), jnp.bfloat16),
+            pltpu.VMEM((4 * freqs, 2 * ntime), jnp.bfloat16),
+            pltpu.SemaphoreType.DMA((5,)),
+            pltpu.SMEM(station_index.shape, jnp.int32),
         ],
         compiler_params=pltpu.CompilerParams(
-            collective_id=0, has_side_effects=True, vmem_limit_bytes=63_000 * 1024
+            collective_id=0, has_side_effects=True, vmem_limit_bytes=32 * 1024 * 1024
         ),
     )(
-        station_index,
         lobe_count,
-        state_in.reshape(whole),
-        base_flow,
-        forcing_in.reshape(whole),
-        right_table(inverse_p.T),
-        right_table(slopes.T),
-        left_table(inverse.transpose(2, 0, 1).reshape(ntime, 2 * freqs)),
-        left_table(forward.reshape(2 * freqs, ntime)),
+        *[
+            pltpu.with_memory_space_constraint(x, pltpu.HBM)
+            for x in (
+                station_index,
+                state_in.reshape(whole),
+                base_flow,
+                forcing_in.reshape(whole),
+                right_table(inverse_p.T),
+                right_table(slopes.T),
+                stacked_table(inverse.transpose(2, 0, 1).reshape(ntime, 2 * freqs)),
+                stacked_table(forward.reshape(2 * freqs, ntime)),
+            )
+        ],
     )
     return tuple(y.reshape(state_in.shape) for y in outs)
 

time: 144 us -> 136 us (0.944); the launches traced: 142 us -> 136 us
  Pallas kernels: 137 us -> 132 us
  local copies, waits for them, and re-layouts: 3.66 us -> 2.11 us
    pallas_call x1, Pallas kernels: 137 us -> 132 us  [per_device_tiled(): pl.pallas_call(functools.partial(relay, dims), out_shape=[jax.ShapeDtypeS...]
    unnamed x4 -> x2, local copies, waits for them, and re-layouts: 3.66 us -> 2.11 us
where the time goes in v3:
time: 136 us
  Pallas kernels  132 us (97%)
  local copies, waits for them, and re-layouts  2.11 us (2%)
    pallas_call x1, Pallas kernels, per_device_tiled(): pl.pallas_call(functools.partial(relay, dims), out_shape=[jax.ShapeDtypeS...  132 us

profile of v3, /device:TPU:30, one launch (start us, length us, event | category | flops | bytes accessed | tf_op | source)
XLA Modules:
  0.0 135.5 jit_solution(18317064388913135803)
XLA Ops:
  1.3 132.1 %shard_map.104 = (f32[4,5,128,128]{3,2,1,0:T(8,128)S(1)}, f32[4,5,128,128]{3,2,1,0:T(8,128)S(1)}) custom-call(s32[1]{0:T(128)S(6)} %copy.13.lobe_ref, s32[2]{0:T(128)} %far_station.1, f32[4,5,128,128]{3,2,1,0:T(8,128)} %bitcast.6, f32[1,5,128,128]{3,2,1,0:T(8,128)} %base_ref.1, f32[4,5,128,128]{3,2,1,0:T(8,128)} %bitcast.7, ...), custom_call_target="tpu_custom_call" | custom-call | tf_op jit(solution)/shard_map/pallas_call | solution.py:1185
  133.4 1.1 copy.14
  134.5 1.1 copy.15

commit v4 on v3

--- a/solution.py
+++ b/solution.py
@@ -663,7 +663,9 @@
     g_state,
     g_forcing,
     r_state,
-    r_base,
+    found,
+    offered,
+    taken,
     s_w,
     plane_w,
     x_one,
@@ -678,7 +680,10 @@
     o_forcing,
     send_sem,
     recv_sem,
-    own_sem,
+    offer_send,
+    offer_recv,
+    w_send,
+    w_recv,
     halo_send,
     halo_recv,
     edge_send,
@@ -703,6 +708,14 @@
     ring = nf * planes
     here = ring_of(me, plane, nf, planes)
     part, block = here // nf, here % nf
+    fold = nf // 2
+    side, seat = me // fold, me % fold
+    share = span // fold
+    blocks = share // own_az
+
+    def mate(i):
+        return side * fold + i, plane
+
 
     def named(device):
         return {"freq": device[0], "plane": device[1]}
@@ -717,18 +730,14 @@
     def greet(device):
         pl.semaphore_signal(barrier, inc=1, device_id=device, device_id_type=MESH)
 
-    @pl.loop(0, nf)
+    @pl.loop(1, fold)
     def _(d):
-        i = (me + nf // 2 + d) % nf
-
-        @pl.when(jnp.logical_not(is_me((i, part))))
-        def _():
-            greet(named((i, part)))
+        greet(named(mate((seat + d) % fold)))
 
     beyond = {"freq": me, "plane": (plane + 1) % planes}
-    behind = {"freq": me, "plane": (plane + planes - 1) % planes}
-    for device in (beyond, right_id, left_id):
-        greet(device)
+    across = {"freq": (1 - side) * fold + seat, "plane": plane}
+    greet(beyond)
+    greet(across)
     load_state = pltpu.make_async_copy(
         state_ref, x_one.at[0, :, :, pl.ds(8, span), :], load_sem.at[0]
     )
@@ -749,7 +758,7 @@
     ]
     for table in tables:
         table.start()
-    pl.semaphore_wait(barrier, nf + 3 - (part == plane).astype(jnp.int32))
+    pl.semaphore_wait(barrier, fold + 1)
 
     def owner(i):
         return device_of(plane * nf + i, nf, planes)
@@ -760,138 +769,180 @@
     def azimuths(i):
         return pl.ds(pl.multiple_of(i * own_az, 8), own_az)
 
-    def mixed(d):
-        return d
-
-    def exchange(k, piece, landing, target, origin, mine):
+    def exchange(k, piece, landing, target, mine, count, landed, sent):
         def copy(i):
             return pltpu.make_async_remote_copy(
                 src_ref=piece(i),
                 dst_ref=landing(mine),
-                send_sem=send_sem.at[k, i],
-                recv_sem=recv_sem.at[k, mine],
+                send_sem=send_sem.at[k],
+                recv_sem=recv_sem.at[k],
                 device_id=named(target(i)),
                 device_id_type=MESH,
             )
 
-        def arrival(i):
-            return pltpu.make_async_remote_copy(
-                src_ref=landing(i),
-                dst_ref=landing(i),
-                send_sem=send_sem.at[k, i],
-                recv_sem=recv_sem.at[k, i],
-                device_id=named(origin(i)),
-                device_id_type=MESH,
-            )
-
-        def own(i):
-            return pltpu.make_async_copy(piece(i), landing(mine), own_sem.at[k])
-
-        def start(first=0, stop=nf):
+        def start(first=0, stop=count):
             @pl.loop(first, stop)
             def _(d):
-                i = (mixed(d) + me) % nf
+                i = (d + me) % count
                 stays = is_me(target(i))
 
                 @pl.when(stays)
                 def _():
-                    own(i).start()
+                    pltpu.make_async_copy(piece(i), landing(mine), recv_sem.at[k]).start()
 
                 @pl.when(jnp.logical_not(stays))
                 def _():
                     copy(i).start()
 
+        def all_of(ref):
+            return pltpu.make_async_remote_copy(
+                src_ref=ref,
+                dst_ref=ref,
+                send_sem=send_sem.at[k],
+                recv_sem=recv_sem.at[k],
+                device_id=beyond,
+                device_id_type=MESH,
+            )
+
         def wait():
-            @pl.loop(0, nf)
-            def _(d):
-                i = (d + me) % nf
-                stays = is_me(target(i))
-
-                @pl.when(stays)
+            all_of(landed).wait_recv()
+
+        def drain():
+            if count < nf:
+                all_of(sent(count - 1)).wait_send()
+            else:
+
+                @pl.when(part == plane)
                 def _():
-                    own(i).wait()
-
-                @pl.when(jnp.logical_not(stays))
+                    all_of(sent(count - 1)).wait_send()
+
+                @pl.when(part != plane)
                 def _():
-                    copy(i).wait_send()
-
-                @pl.when(jnp.logical_not(is_me(origin(i))))
-                def _():
-                    arrival(i).wait_recv()
-
-        return start, wait
-
-    base_start, base_wait = exchange(
+                    all_of(sent(count)).wait_send()
+
+        return start, wait, drain
+
+    def chunk(i):
+        return pl.ds(pl.multiple_of(i * share, 8), share)
+
+    base_start, base_wait, base_drain = exchange(
         0,
-        lambda i: base_ref.at[:, :, azimuths(i), :],
-        lambda j: r_base.at[j],
-        owner,
-        holder,
-        me,
+        lambda i: base_ref.at[:, :, chunk(i), :],
+        lambda j: found.at[j],
+        mate,
+        seat,
+        fold,
+        found,
+        lambda n: found.at[pl.ds(0, n)],
     )
-    groups = [(v, min(v + GROUP, variables)) for v in range(0, variables, GROUP)]
-
-    def w_moves(g):
-        first, stop = groups[g]
+
+    def offers(station, v):
+        return pltpu.make_async_remote_copy(
+            src_ref=offered.at[station, v],
+            dst_ref=taken.at[station, v],
+            send_sem=offer_send.at[station, v],
+            recv_sem=offer_recv.at[station, v],
+            device_id=across,
+            device_id_type=MESH,
+        )
+
+    def w_moves(station, v):
         return exchange(
-            1 + g,
-            lambda i: s_w.at[0, pl.ds(first, stop - first)],
-            lambda j: plane_w.at[0, pl.ds(first, stop - first), azimuths(j), :],
-            holder,
-            owner,
-            block,
+            1 + station * variables + v,
+            lambda i: s_w.at[station, v],
+            lambda j: plane_w.at[station, v, chunk(j), :],
+            mate,
+            seat,
+            fold,
+            plane_w.at[station, v],
+            lambda n: plane_w.at[station, v, pl.ds(0, n * share), :],
         )
 
-    later_start, later_wait = exchange(
-        2 + 3 * variables,
-        lambda i: s_w.at[1, pl.ds(0, RETURNED)],
-        lambda j: plane_w.at[1, pl.ds(0, RETURNED), azimuths(j), :],
-        holder,
-        owner,
-        block,
-    )
-
-    def march_moves(v):
-        return exchange(
-            3 + 3 * variables + v,
-            lambda i: o_march.at[i, v],
-            lambda j: b_one.at[:, v, azimuths(j), :],
-            holder,
-            owner,
-            block,
+    def coefficient_copies():
+        for j in range(blocks):
+            target = device_of(plane * nf + seat * blocks + j, nf, planes)
+            source = s_w.at[1, :, pl.ds(j * own_az, own_az), :]
+            remote = pltpu.make_async_remote_copy(
+                src_ref=source,
+                dst_ref=w_ref,
+                send_sem=w_send.at[j],
+                recv_sem=w_recv.at[0],
+                device_id=named(target),
+                device_id_type=MESH,
+            )
+            local = pltpu.make_async_copy(source, w_ref, w_recv.at[1])
+            near = target[0] // fold == side
+            yield remote, local, near & jnp.logical_not(is_me(target)), near & is_me(target)
+
+    def coefficient_start():
+        for remote, local, away, home in coefficient_copies():
+            pl.when(away)(remote.start)
+            pl.when(home)(local.start)
+
+    def coefficient_wait():
+        for remote, local, away, home in coefficient_copies():
+            pl.when(away)(remote.wait_send)
+            pl.when(home)(local.wait)
+        source = (side * fold + block // blocks, part)
+        arrived = pltpu.make_async_remote_copy(
+            src_ref=w_ref,
+            dst_ref=w_ref,
+            send_sem=w_send.at[0],
+            recv_sem=w_recv.at[0],
+            device_id=named(source),
+            device_id_type=MESH,
         )
+        pl.when(jnp.logical_not(is_me(source)))(arrived.wait_recv)
 
     settled = SWEEPS % 2
 
     def state_moves(v):
         return exchange(
-            1 + variables + v,
+            1 + 2 * variables + v,
             lambda i: x_one.at[
                 settled, :, v, pl.ds(pl.multiple_of(8 + i * own_az, 8), own_az), :
             ],
             lambda j: r_state.at[j, v],
             owner,
+            me,
+            nf,
+            r_state.at[:, v],
+            lambda n: r_state.at[pl.ds(0, n), v],
+        )
+
+    def march_moves(v):
+        return exchange(
+            1 + 4 * variables + v,
+            lambda i: o_march.at[i, v],
+            lambda j: b_one.at[:, v, azimuths(j), :],
             holder,
-            me,
+            block,
+            nf,
+            b_one.at[:, v],
+            lambda n: o_march.at[pl.ds(0, n), v],
         )
 
     def out_moves(v):
         return exchange(
-            1 + 2 * variables + v,
+            1 + 3 * variables + v,
             lambda i: o_state.at[i, v],
             lambda j: g_state.at[:, v, azimuths(j), :],
             holder,
-            owner,
             block,
+            nf,
+            g_state.at[:, v],
+            lambda n: o_state.at[pl.ds(0, n), v],
         )
 
-    forcing_start, forcing_wait = exchange(
-        1 + 3 * variables,
+    forcing_start, forcing_wait, forcing_drain = exchange(
+        1 + 4 * variables + RETURNED,
         lambda i: o_forcing.at[i],
         lambda j: g_forcing.at[:, :, azimuths(j), :],
         holder,
-        owner,
         block,
+        nf,
+        g_forcing,
+        lambda n: o_forcing.at[pl.ds(0, n)],
     )
     base_start()
 
@@ -902,8 +953,8 @@
             pltpu.make_async_remote_copy(
                 src_ref=x_ref.at[slot, source, rows, :],
                 dst_ref=x_ref.at[slot, target, rows, :],
-                send_sem=halo_send.at[side, e, v],
-                recv_sem=halo_recv.at[side, e, v],
+                send_sem=halo_send.at[side, slot, v],
+                recv_sem=halo_recv.at[side, slot, v],
                 device_id=device,
                 device_id_type=MESH,
             )
@@ -913,25 +964,23 @@
             )
         ]
 
-    def edge_copies(e, v):
-        return [
-            pltpu.make_async_remote_copy(
-                src_ref=edge_out.at[e, v, side],
-                dst_ref=edge_in.at[e, v, side],
-                send_sem=edge_send.at[side, e, v],
-                recv_sem=edge_recv.at[side, e, v],
-                device_id=target,
-                device_id_type=MESH,
-            )
-            for side, target in ((0, beyond), (1, behind))
-        ]
-
-    def send_edges(slot, e, v):
+    def edge_copy(e, v):
+        turn = e % 2
+        return pltpu.make_async_remote_copy(
+            src_ref=edge_out.at[turn, v],
+            dst_ref=edge_in.at[turn, v],
+            send_sem=edge_send.at[turn, v],
+            recv_sem=edge_recv.at[turn, v],
+            device_id=beyond,
+            device_id_type=MESH,
+        )
+
+    def send_edges(e, v):
+        slot = e % 2
         for ck in range(parts):
-            edge_out[e, v, 0, pl.ds(ck, 1), :] = x_one[slot, ck, v, pl.ds(7 + span, 1), :]
-            edge_out[e, v, 1, pl.ds(ck, 1), :] = x_one[slot, ck, v, pl.ds(8, 1), :]
-        for copy in edge_copies(e, v):
-            copy.start()
+            edge_out[slot, v, pl.ds(ck, 1), :] = x_one[slot, ck, v, pl.ds(7 + span, 1), :]
+            edge_out[slot, v, pl.ds(parts + ck, 1), :] = x_one[slot, ck, v, pl.ds(8, 1), :]
+        edge_copy(e, v).start()
 
     for kk in range(per_dev):
         modes = lax.broadcasted_iota(jnp.int32, (nf, radii), 0) * per_dev + kk
@@ -940,7 +989,7 @@
 
     @pl.loop(0, variables)
     def _(v):
-        send_edges(0, 0, v)
+        send_edges(0, v)
 
     load_forcing.wait()
 
@@ -951,32 +1000,31 @@
 
     for table in tables:
         table.wait()
-    position = here * own_az + lax.broadcasted_iota(jnp.int32, (own_az, radii), 0)
+    position = plane * span + seat * share + lax.broadcasted_iota(jnp.int32, (share, radii), 0)
     phases = (lobe_ref[0] * position) % (span * planes)
     shape = 1.0 + 0.5 * jnp.cos(2.0 * math.pi * phases.astype(jnp.float32) / (span * planes))
     base_wait()
-
-    def coefficient(station, v):
+    for station in range(STEPS):
         wanted = station_ref[station]
-        return (BASE_SCALE * shape) * r_base[wanted // stored, wanted % stored, v]
-
-    for g, (first, stop) in enumerate(groups):
-        for v in range(first, stop):
-            s_w[0, v] = coefficient(0, v)
-        w_moves(g)[0]()
-    for v in range(variables):
-        w_ref[v] = coefficient(1, v)
-        if v < RETURNED:
-            s_w[1, v] = coefficient(1, v)
-    later_start()
+        for v in range(variables):
+            offered[station, v] = (BASE_SCALE * shape) * found[
+                (wanted // stored) % fold, wanted % stored, v
+            ]
+            offers(station, v).start()
+    for station in range(STEPS):
+        ours = jnp.full((share, radii), station_ref[station] // (stored * fold)) == side
+        for v in range(variables):
+            offers(station, v).wait()
+            s_w[station, v] = jnp.where(ours, offered[station, v], taken[station, v])
+            if station == 0 or v < RETURNED:
+                w_moves(station, v)[0]()
 
     def sweep_plane(e, v, w):
         src, dst = e % 2, (e + 1) % 2
-        for copy in edge_copies(e, v):
-            copy.wait()
+        edge_copy(e, v).wait()
         for ck in range(parts):
-            x_one[src, ck, v, pl.ds(7, 1), :] = edge_in[e, v, 0, pl.ds(ck, 1), :]
-            x_one[src, ck, v, pl.ds(8 + span, 1), :] = edge_in[e, v, 1, pl.ds(ck, 1), :]
+            x_one[src, ck, v, pl.ds(7, 1), :] = edge_in[src, v, pl.ds(ck, 1), :]
+            x_one[src, ck, v, pl.ds(8 + span, 1), :] = edge_in[src, v, pl.ds(parts + ck, 1), :]
         for kk in range(per_dev):
             rate = (me * per_dev + kk).astype(jnp.float32) * (0.5 / freqs)
             at = [c * per_dev + kk for c in range(2)]
@@ -993,21 +1041,29 @@
             x_one[dst, at[0], v, pl.ds(8, span), :] = q[:span]
             x_one[dst, at[1], v, pl.ds(8, span), :] = q[span:]
 
-    for g, (first, stop) in enumerate(groups):
-        w_moves(g)[1]()
-
-        @pl.loop(0, SWEEPS * (stop - first))
-        def _(turn):
-            e, v = turn // (stop - first), first + turn % (stop - first)
-            sweep_plane(e, v, plane_w[0, v])
-
-            @pl.when((e < SWEEPS - 1) | (v < RETURNED))
+    @pl.loop(0, SWEEPS + LAG * (variables - 1))
+    def _(turn):
+        @pl.loop(0, variables)
+        def _(v):
+            e = turn - LAG * v
+
+            @pl.when((e >= 0) & (e < SWEEPS))
             def _():
-                send_edges((e + 1) % 2, e + 1, v)
-
-            @pl.when(e == SWEEPS - 1)
-            def _():
-                state_moves(v)[0]()
+                @pl.when(e == 0)
+                def _():
+                    w_moves(0, v)[1]()
+
+                sweep_plane(e, v, plane_w[0, v])
+
+                @pl.when((e < SWEEPS - 1) | (v < RETURNED))
+                def _():
+                    send_edges(e + 1, v)
+
+                @pl.when(e == SWEEPS - 1)
+                def _():
+                    state_moves(v)[0]()
+
+    coefficient_start()
 
     def each_run(v, visit):
         for c in range(2):
@@ -1096,6 +1152,7 @@
             advect_slab(slot, side * (own_az - 1), final)
 
     advect_all(0, False)
+    coefficient_wait()
 
     @pl.loop(0, SWEEPS * variables)
     def _(turn):
@@ -1128,9 +1185,10 @@
 
     advect_all(SWEEPS, True)
     forcing_start()
-    later_wait()
     for v in range(RETURNED):
+        w_moves(1, v)[1]()
         march_moves(v)[1]()
+        state_moves(v)[2]()
 
     @pl.loop(0, SWEEPS * RETURNED)
     def _(turn):
@@ -1139,7 +1197,7 @@
 
         @pl.when(e < 2 * SWEEPS - 1)
         def _():
-            send_edges((e + 1) % 2, e + 1, v)
+            send_edges(e + 1, v)
 
     out_state = pltpu.make_async_copy(
         x_one.at[0, :, pl.ds(0, RETURNED), pl.ds(8, span), :],
@@ -1153,11 +1211,25 @@
         out_moves(v)[1]()
 
     out_state.wait()
-
     forcing_wait()
-
-
-GROUP = 1
+    base_drain()
+    for v in range(RETURNED):
+        w_moves(1, v)[2]()
+        march_moves(v)[2]()
+
+    @pl.loop(0, variables)
+    def _(v):
+        w_moves(0, v)[2]()
+
+    @pl.loop(RETURNED, variables)
+    def _(v):
+        state_moves(v)[2]()
+        out_moves(v)[2]()
+
+    forcing_drain()
+
+
+LAG = 2
 RETURNED = 1
 
 
@@ -1174,14 +1246,14 @@
     inverse, forward = transform_tables(mode_ids, freqs, ntime)
     dims = (nf, planes, own_az, variables, per_dev, radii, stored)
     parts = 2 * per_dev
-    edge_rows = -(-parts // 8) * 8
+    edge_rows = -(-2 * parts // 8) * 8
     anywhere = pl.BlockSpec(memory_space=pl.ANY)
     far = pl.BlockSpec(memory_space=pltpu.HBM)
     f32 = jnp.float32
     whole = (parts, variables, span_az, radii)
     slab = variables * 2 * freqs
-    moves = 3 + 3 * variables + RETURNED
-    rounds = 2 * SWEEPS
+    share = span_az // (nf // 2)
+    moves = 2 + 4 * variables + RETURNED
     outs = pl.pallas_call(
         functools.partial(relay, dims),
         out_shape=[jax.ShapeDtypeStruct(whole, f32)] * 2,
@@ -1189,26 +1261,31 @@
         out_specs=[anywhere, anywhere],
         scratch_shapes=[
             pltpu.VMEM((nf, variables, parts, own_az, radii), f32),
-            pltpu.VMEM((nf, stored, variables, own_az, radii), f32),
-            pltpu.VMEM((2, variables, own_az, radii), f32),
-            pltpu.VMEM((2, variables, span_az, radii), f32),
+            pltpu.VMEM((nf // 2, stored, variables, share, radii), f32),
+            pltpu.VMEM((STEPS, variables, share, radii), f32),
+            pltpu.VMEM((STEPS, variables, share, radii), f32),
+            pltpu.VMEM((STEPS, variables, share, radii), f32),
+            pltpu.VMEM((STEPS, variables, span_az, radii), f32),
             pltpu.VMEM((2, parts, variables, span_az + 16, radii), f32),
             pltpu.VMEM(whole, f32),
-            pltpu.VMEM((rounds, variables, 2, edge_rows, radii), f32),
-            pltpu.VMEM((rounds, variables, 2, edge_rows, radii), f32),
+            pltpu.VMEM((2, variables, edge_rows, radii), f32),
+            pltpu.VMEM((2, variables, edge_rows, radii), f32),
             pltpu.VMEM((2, own_az + 2, slab, radii), f32),
             pltpu.VMEM((own_az, slab, radii), f32),
             pltpu.VMEM((variables, own_az, radii), f32),
             pltpu.VMEM((nf, variables, parts, own_az, radii), f32),
             pltpu.VMEM((nf, RETURNED, parts, own_az, radii), f32),
             pltpu.VMEM((nf, parts, variables, own_az, radii), f32),
-            pltpu.SemaphoreType.DMA((moves, nf)),
-            pltpu.SemaphoreType.DMA((moves, nf)),
             pltpu.SemaphoreType.DMA((moves,)),
-            pltpu.SemaphoreType.DMA((2, SWEEPS + 1, variables)),
-            pltpu.SemaphoreType.DMA((2, SWEEPS + 1, variables)),
-            pltpu.SemaphoreType.DMA((2, rounds, variables)),
-            pltpu.SemaphoreType.DMA((2, rounds, variables)),
+            pltpu.SemaphoreType.DMA((moves,)),
+            pltpu.SemaphoreType.DMA((STEPS, variables)),
+            pltpu.SemaphoreType.DMA((STEPS, variables)),
+            pltpu.SemaphoreType.DMA((share // own_az,)),
+            pltpu.SemaphoreType.DMA((2,)),
+            pltpu.SemaphoreType.DMA((2, 2, variables)),
+            pltpu.SemaphoreType.DMA((2, 2, variables)),
+            pltpu.SemaphoreType.DMA((2, variables)),
+            pltpu.SemaphoreType.DMA((2, variables)),
             pltpu.SemaphoreType.DMA((2,)),
             pltpu.VMEM((freqs, radii), f32),
             pltpu.VMEM((2 * radii, 2 * radii), jnp.bfloat16),
@@ -1241,7 +1318,8 @@
 
 
 def per_device_any(*args):
-    tiles = args[0].shape[3] % (8 * lax.axis_size("freq")) == 0
+    nf = lax.axis_size("freq")
+    tiles = args[0].shape[3] % (8 * nf) == 0 and nf % 2 == 0 and lax.axis_size("plane") == 2
     return (per_device_tiled if tiles else per_device)(*args)
 
 

time: 136 us -> 127 us (0.934)
  Pallas kernels: 132 us -> 123 us
    pallas_call x1, Pallas kernels: 132 us -> 123 us  [per_device_tiled(): pl.pallas_call(functools.partial(relay, dims), out_shape=[jax.ShapeDtypeS...]
where the time goes in v4:
time: 127 us; the launch traced here: 126 us
  Pallas kernels  123 us (97%)
  local copies, waits for them, and re-layouts  2.11 us (2%)
  between operations  1.29 us (1%)
    pallas_call x1, Pallas kernels, per_device_tiled(): pl.pallas_call(functools.partial(relay, dims), out_shape=[jax.ShapeDtypeS...  123 us

profile of v4, /device:TPU:30, one launch (start us, length us, event | category | flops | bytes accessed | tf_op | source)
XLA Modules:
  0.0 126.3 jit_solution(10296923073262980436)
XLA Ops:
  1.3 122.9 %shard_map.104 = (f32[4,5,128,128]{3,2,1,0:T(8,128)S(1)}, f32[4,5,128,128]{3,2,1,0:T(8,128)S(1)}) custom-call(s32[1]{0:T(128)S(6)} %copy.13.lobe_ref, s32[2]{0:T(128)} %far_station.1, f32[4,5,128,128]{3,2,1,0:T(8,128)} %bitcast.6, f32[1,5,128,128]{3,2,1,0:T(8,128)} %base_ref.1, f32[4,5,128,128]{3,2,1,0:T(8,128)} %bitcast.7, ...), custom_call_target="tpu_custom_call" | custom-call | tf_op jit(solution)/shard_map/pallas_call | solution.py:1257
  124.2 1.1 copy.14
  125.3 1.1 copy.15

commit v5 on v4

--- a/solution.py
+++ b/solution.py
@@ -660,8 +660,7 @@
     far_st,
     far_inv,
     far_fwd,
-    g_state,
-    g_forcing,
+    g_both,
     r_state,
     found,
     offered,
@@ -698,6 +697,7 @@
     station_ref,
 ):
     nf, planes, own_az, variables, per_dev, radii, stored = dims
+    g_state, g_forcing = g_both.at[0], g_both.at[1]
     freqs = nf * per_dev
     span = nf * own_az
     parts = 2 * per_dev
@@ -1004,20 +1004,27 @@
     phases = (lobe_ref[0] * position) % (span * planes)
     shape = 1.0 + 0.5 * jnp.cos(2.0 * math.pi * phases.astype(jnp.float32) / (span * planes))
     base_wait()
-    for station in range(STEPS):
+
+    def offer(station):
         wanted = station_ref[station]
         for v in range(variables):
             offered[station, v] = (BASE_SCALE * shape) * found[
                 (wanted // stored) % fold, wanted % stored, v
             ]
             offers(station, v).start()
-    for station in range(STEPS):
+
+    def settle(station, gathered):
         ours = jnp.full((share, radii), station_ref[station] // (stored * fold)) == side
         for v in range(variables):
             offers(station, v).wait()
             s_w[station, v] = jnp.where(ours, offered[station, v], taken[station, v])
-            if station == 0 or v < RETURNED:
+            if v < gathered:
                 w_moves(station, v)[0]()
+
+    offer(0)
+    settle(0, variables)
+    for station in range(1, STEPS):
+        offer(station)
 
     def sweep_plane(e, v, w):
         src, dst = e % 2, (e + 1) % 2
@@ -1063,6 +1070,8 @@
                 def _():
                     state_moves(v)[0]()
 
+    for station in range(1, STEPS):
+        settle(station, RETURNED)
     coefficient_start()
 
     def each_run(v, visit):
@@ -1256,9 +1265,9 @@
     moves = 2 + 4 * variables + RETURNED
     outs = pl.pallas_call(
         functools.partial(relay, dims),
-        out_shape=[jax.ShapeDtypeStruct(whole, f32)] * 2,
+        out_shape=jax.ShapeDtypeStruct((2, *whole), f32),
         in_specs=[pl.BlockSpec(memory_space=pltpu.SMEM)] + [far] * 8,
-        out_specs=[anywhere, anywhere],
+        out_specs=anywhere,
         scratch_shapes=[
             pltpu.VMEM((nf, variables, parts, own_az, radii), f32),
             pltpu.VMEM((nf // 2, stored, variables, share, radii), f32),
@@ -1314,7 +1323,7 @@
             )
         ],
     )
-    return tuple(y.reshape(state_in.shape) for y in outs)
+    return tuple(outs[n].reshape(state_in.shape) for n in range(2))
 
 
 def per_device_any(*args):

time: 127 us -> 127 us (level)
    unnamed x2 -> x0, local copies, waits for them, and re-layouts: 2.11 us -> none
    slice x0 -> x1, local copies, waits for them, and re-layouts: none -> 1.79 us  [per_device_tiled(): return tuple((outs[n].reshape(state_in.shape) for n in range(2)))]
where the time goes in v5:
time: 127 us; the launch traced here: 126 us
  Pallas kernels  123 us (97%)
  local copies, waits for them, and re-layouts  1.79 us (1%)
  between operations  1.29 us (1%)
    pallas_call x1, Pallas kernels, per_device_tiled(): pl.pallas_call(functools.partial(relay, dims), out_shape=jax.ShapeDtypeSt...  123 us

profile of v5, /device:TPU:30, one launch (start us, length us, event | category | flops | bytes accessed | tf_op | source)
XLA Modules:
  0.0 125.9 jit_solution(2546928673339504934)
XLA Ops:
  1.3 122.8 %shard_map.104 = f32[2,4,5,128,128]{4,3,2,1,0:T(8,128)S(1)} custom-call(s32[1]{0:T(128)S(6)} %copy.11.lobe_ref, s32[2]{0:T(128)} %far_station.1, f32[4,5,128,128]{3,2,1,0:T(8,128)} %bitcast.6, f32[1,5,128,128]{3,2,1,0:T(8,128)} %base_ref.1, f32[4,5,128,128]{3,2,1,0:T(8,128)} %bitcast.7, bf16[256,256]{1,0:T(8,128)(2,1)} %constant.8.clone.far_qt, ...), custom_call_target="tpu_custom_call" | custom-call | tf_op jit(solution)/shard_map/pallas_call | solution.py:1266
  124.1 1.8 %fusion = (f32[1,4,5,128,128]{4,3,2,1,0:T(8,128)}, f32[1,4,5,128,128]{4,3,2,1,0:T(8,128)}) fusion(f32[2,4,5,128,128]{4,3,2,1,0:T(8,128)S(1)} %shard_map.104), kind=kLoop, calls=%fused_computation | loop fusion | bytes 5242880 | tf_op jit(solution)/shard_map/slice | solution.py:1326

commit v6 on v5

--- a/solution.py
+++ b/solution.py
@@ -662,7 +662,8 @@
     far_fwd,
     g_both,
     r_state,
-    found,
+    found_first,
+    found_rest,
     offered,
     taken,
     s_w,
@@ -825,16 +826,19 @@
     def chunk(i):
         return pl.ds(pl.multiple_of(i * share, 8), share)
 
-    base_start, base_wait, base_drain = exchange(
-        0,
-        lambda i: base_ref.at[:, :, chunk(i), :],
-        lambda j: found.at[j],
-        mate,
-        seat,
-        fold,
-        found,
-        lambda n: found.at[pl.ds(0, n)],
-    )
+    def base_moves(n):
+        some = (pl.ds(0, FIRST), pl.ds(FIRST, variables - FIRST))[n]
+        found = (found_first, found_rest)[n]
+        return exchange(
+            n * (2 + 4 * variables + RETURNED),
+            lambda i: base_ref.at[:, some, chunk(i), :],
+            lambda j: found.at[j],
+            mate,
+            seat,
+            fold,
+            found,
+            lambda count: found.at[pl.ds(0, count)],
+        )
 
     def offers(station, v):
         return pltpu.make_async_remote_copy(
@@ -944,7 +948,8 @@
         g_forcing,
         lambda n: o_forcing.at[pl.ds(0, n)],
     )
-    base_start()
+    for n in range(2):
+        base_moves(n)[0]()
 
     def halo_copies(e, v):
         slot = e % 2
@@ -1003,13 +1008,12 @@
     position = plane * span + seat * share + lax.broadcasted_iota(jnp.int32, (share, radii), 0)
     phases = (lobe_ref[0] * position) % (span * planes)
     shape = 1.0 + 0.5 * jnp.cos(2.0 * math.pi * phases.astype(jnp.float32) / (span * planes))
-    base_wait()
-
-    def offer(station):
+    def offer(station, first, stop):
         wanted = station_ref[station]
-        for v in range(variables):
+        for v in range(first, stop):
+            found, at = (found_first, v) if v < FIRST else (found_rest, v - FIRST)
             offered[station, v] = (BASE_SCALE * shape) * found[
-                (wanted // stored) % fold, wanted % stored, v
+                (wanted // stored) % fold, wanted % stored, at
             ]
             offers(station, v).start()
 
@@ -1021,32 +1025,60 @@
             if v < gathered:
                 w_moves(station, v)[0]()
 
-    offer(0)
+    base_moves(0)[1]()
+    offer(0, 0, FIRST)
+    base_moves(1)[1]()
+    offer(0, FIRST, variables)
     settle(0, variables)
     for station in range(1, STEPS):
-        offer(station)
-
-    def sweep_plane(e, v, w):
+        offer(station, 0, variables)
+
+    def sweep_rows(src, v, w, first, size):
+        here = pl.ds(first, size)
+        above, below = pl.ds(first - 1, size), pl.ds(first + 1, size)
+        summed = []
+        for kk in range(per_dev):
+            rate = (me * per_dev + kk).astype(jnp.float32) * (0.5 / freqs)
+            at = [c * per_dev + kk for c in range(2)]
+            real, imag = [x_one[src, ck, v, here, :] for ck in at]
+            mixing = (w * real - rate * imag, w * imag + rate * real)
+            summed.append(
+                [
+                    SIDE_WEIGHT * (x_one[src, ck, v, above, :] + x_one[src, ck, v, below, :])
+                    + b_one[ck, v, pl.ds(first - 8, size), :]
+                    - mixed
+                    for ck, mixed in zip(at, mixing)
+                ]
+            )
+        return summed
+
+    def sweep_plane(e, v, station, last):
         src, dst = e % 2, (e + 1) % 2
         edge_copy(e, v).wait()
         for ck in range(parts):
             x_one[src, ck, v, pl.ds(7, 1), :] = edge_in[src, v, pl.ds(ck, 1), :]
             x_one[src, ck, v, pl.ds(8 + span, 1), :] = edge_in[src, v, pl.ds(parts + ck, 1), :]
-        for kk in range(per_dev):
-            rate = (me * per_dev + kk).astype(jnp.float32) * (0.5 / freqs)
-            at = [c * per_dev + kk for c in range(2)]
-            real, imag = [x_one[src, ck, v, pl.ds(8, span), :] for ck in at]
-            mixing = (w * real - rate * imag, w * imag + rate * real)
-            summed = [
-                SIDE_WEIGHT
-                * (x_one[src, ck, v, pl.ds(7, span), :] + x_one[src, ck, v, pl.ds(9, span), :])
-                + b_one[ck, v]
-                - mixed_in
-                for ck, mixed_in in zip(at, mixing)
-            ]
+
+        @pl.when(jnp.logical_not(last))
+        def _():
+            tiles = []
+            for first in (span, 8):
+                w = plane_w[station, v, pl.ds(first - 8, 8), :]
+                for pair_of in sweep_rows(src, v, w, first, 8):
+                    tiles += pair_of
+            q = times_right(jnp.concatenate(tiles, axis=0), qt_ref[...])
+            for kk in range(per_dev):
+                for c in range(2):
+                    ck, n = c * per_dev + kk, 8 * (2 * kk + c)
+                    edge_out[dst, v, pl.ds(ck, 1), :] = q[n + 7 : n + 8]
+                    n += 8 * parts
+                    edge_out[dst, v, pl.ds(parts + ck, 1), :] = q[n : n + 1]
+            edge_copy(e + 1, v).start()
+
+        for kk, summed in enumerate(sweep_rows(src, v, plane_w[station, v], 8, span)):
             q = times_right(jnp.concatenate(summed, axis=0), qt_ref[...])
-            x_one[dst, at[0], v, pl.ds(8, span), :] = q[:span]
-            x_one[dst, at[1], v, pl.ds(8, span), :] = q[span:]
+            x_one[dst, kk, v, pl.ds(8, span), :] = q[:span]
+            x_one[dst, per_dev + kk, v, pl.ds(8, span), :] = q[span:]
 
     @pl.loop(0, SWEEPS + LAG * (variables - 1))
     def _(turn):
@@ -1060,11 +1092,7 @@
                 def _():
                     w_moves(0, v)[1]()
 
-                sweep_plane(e, v, plane_w[0, v])
-
-                @pl.when((e < SWEEPS - 1) | (v < RETURNED))
-                def _():
-                    send_edges(e + 1, v)
+                sweep_plane(e, v, 0, (e == SWEEPS - 1) & (v >= RETURNED))
 
                 @pl.when(e == SWEEPS - 1)
                 def _():
@@ -1202,11 +1230,7 @@
     @pl.loop(0, SWEEPS * RETURNED)
     def _(turn):
         e, v = SWEEPS + turn // RETURNED, turn % RETURNED
-        sweep_plane(e, v, plane_w[1, v])
-
-        @pl.when(e < 2 * SWEEPS - 1)
-        def _():
-            send_edges(e + 1, v)
+        sweep_plane(e, v, 1, e == 2 * SWEEPS - 1)
 
     out_state = pltpu.make_async_copy(
         x_one.at[0, :, pl.ds(0, RETURNED), pl.ds(8, span), :],
@@ -1221,7 +1245,8 @@
 
     out_state.wait()
     forcing_wait()
-    base_drain()
+    for n in range(2):
+        base_moves(n)[2]()
     for v in range(RETURNED):
         w_moves(1, v)[2]()
         march_moves(v)[2]()
@@ -1239,6 +1264,7 @@
 
 
 LAG = 2
+FIRST = 1
 RETURNED = 1
 
 
@@ -1262,7 +1288,7 @@
     whole = (parts, variables, span_az, radii)
     slab = variables * 2 * freqs
     share = span_az // (nf // 2)
-    moves = 2 + 4 * variables + RETURNED
+    moves = 3 + 4 * variables + RETURNED
     outs = pl.pallas_call(
         functools.partial(relay, dims),
         out_shape=jax.ShapeDtypeStruct((2, *whole), f32),
@@ -1270,7 +1296,8 @@
         out_specs=anywhere,
         scratch_shapes=[
             pltpu.VMEM((nf, variables, parts, own_az, radii), f32),
-            pltpu.VMEM((nf // 2, stored, variables, share, radii), f32),
+            pltpu.VMEM((nf // 2, stored, FIRST, share, radii), f32),
+            pltpu.VMEM((nf // 2, stored, variables - FIRST, share, radii), f32),
             pltpu.VMEM((STEPS, variables, share, radii), f32),
             pltpu.VMEM((STEPS, variables, share, radii), f32),
             pltpu.VMEM((STEPS, variables, share, radii), f32),

time: 127 us -> 125 us (0.984)
  Pallas kernels: 123 us -> 121 us
    pallas_call x1, Pallas kernels: 123 us -> 121 us  [per_device_tiled(): pl.pallas_call(functools.partial(relay, dims), out_shape=jax.ShapeDtypeSt...]
where the time goes in v6:
time: 125 us; the launch traced here: 124 us
  Pallas kernels  121 us (97%)
  local copies, waits for them, and re-layouts  1.79 us (1%)
  between operations  1.29 us (1%)
    pallas_call x1, Pallas kernels, per_device_tiled(): pl.pallas_call(functools.partial(relay, dims), out_shape=jax.ShapeDtypeSt...  121 us

profile of v6, /device:TPU:30, one launch (start us, length us, event | category | flops | bytes accessed | tf_op | source)
XLA Modules:
  0.0 124.1 jit_solution(3183357385138163825)
XLA Ops:
  1.3 121.0 %shard_map.104 = f32[2,4,5,128,128]{4,3,2,1,0:T(8,128)S(1)} custom-call(s32[1]{0:T(128)S(6)} %copy.11.lobe_ref, s32[2]{0:T(128)} %far_station.1, f32[4,5,128,128]{3,2,1,0:T(8,128)} %bitcast.6, f32[1,5,128,128]{3,2,1,0:T(8,128)} %base_ref.1, f32[4,5,128,128]{3,2,1,0:T(8,128)} %bitcast.7, bf16[256,256]{1,0:T(8,128)(2,1)} %constant.8.clone.far_qt, ...), custom_call_target="tpu_custom_call" | custom-call | tf_op jit(solution)/shard_map/pallas_call | solution.py:1292
  122.3 1.8 %fusion = (f32[1,4,5,128,128]{4,3,2,1,0:T(8,128)}, f32[1,4,5,128,128]{4,3,2,1,0:T(8,128)}) fusion(f32[2,4,5,128,128]{4,3,2,1,0:T(8,128)S(1)} %shard_map.104), kind=kLoop, calls=%fused_computation | loop fusion | bytes 5242880 | tf_op jit(solution)/shard_map/slice | solution.py:1353

commit v7 on v6

--- a/solution.py
+++ b/solution.py
@@ -1193,7 +1193,7 @@
 
     @pl.loop(0, SWEEPS * variables)
     def _(turn):
-        e, v = turn // variables, turn % variables
+        e, v = turn // variables, (turn + RETURNED) % variables
 
         @pl.when(e > 0)
         def _():

time: 125 us -> 125 us (level)
  no operation moved by 1% of the time
where the time goes in v7:
time: 125 us; the launch traced here: 124 us
  Pallas kernels  121 us (97%)
  local copies, waits for them, and re-layouts  1.79 us (1%)
  between operations  1.29 us (1%)
    pallas_call x1, Pallas kernels, per_device_tiled(): pl.pallas_call(functools.partial(relay, dims), out_shape=jax.ShapeDtypeSt...  121 us

profile of v7, /device:TPU:30, one launch (start us, length us, event | category | flops | bytes accessed | tf_op | source)
XLA Modules:
  0.0 124.2 jit_solution(4120981245278132222)
XLA Ops:
  1.3 121.1 %shard_map.104 = f32[2,4,5,128,128]{4,3,2,1,0:T(8,128)S(1)} custom-call(s32[1]{0:T(128)S(6)} %copy.11.lobe_ref, s32[2]{0:T(128)} %far_station.1, f32[4,5,128,128]{3,2,1,0:T(8,128)} %bitcast.6, f32[1,5,128,128]{3,2,1,0:T(8,128)} %base_ref.1, f32[4,5,128,128]{3,2,1,0:T(8,128)} %bitcast.7, bf16[256,256]{1,0:T(8,128)(2,1)} %constant.8.clone.far_qt, ...), custom_call_target="tpu_custom_call" | custom-call | tf_op jit(solution)/shard_map/pallas_call | solution.py:1292
  122.4 1.8 %fusion = (f32[1,4,5,128,128]{4,3,2,1,0:T(8,128)}, f32[1,4,5,128,128]{4,3,2,1,0:T(8,128)}) fusion(f32[2,4,5,128,128]{4,3,2,1,0:T(8,128)S(1)} %shard_map.104), kind=kLoop, calls=%fused_computation | loop fusion | bytes 5242880 | tf_op jit(solution)/shard_map/slice | solution.py:1353
